TPU v7x, 32 devices: a whole 2x2x4 slice. The times are simulated.
32 devices in a mesh: streams: 8 (over z, x), tm: 4 (over y, core).
Axes of the slice: x: 2, y: 2, z: 4, core: 2. Of those that a mesh axis runs over, the one named last changes fastest.
Arguments:
- signal: float32 [2, 2097152], P(None, ('streams', 'tm')), parts along dimension 1, may hold values from -6 to 6
- coarse_taps: float32 [16, 64], replicated, may hold values from -1.5 to 1.5
- fine_taps: float32 [12, 512], replicated, may hold values from -1.8 to 1.8
Outputs:
- channelized: float32 [2, 64, 64, 512], P(None, 'tm', 'streams'), parts along dimension 2
There are 8 independent parts, one for each index of `streams`. A program takes and returns all parts, laid end to end along the dimension named above; an argument that names none is the same for every part. Nothing has to cross between parts.
All inputs are finite; a program needn't handle non-finite values.
Results may differ from a plain program's by a relative error of at most 0.00007.
Values sent between devices are 32-bit elements; how exact they have to be, the bound alone decides.
No kernel may reach another device: no remote copies, remote signals or barrier semaphores. Data moves between devices by JAX's collectives and lax.ppermute only.
A program may use at most 320 MiB of HBM per device.

v0:
```python
import math

import jax
import jax.numpy as jnp
from jax import lax
from jax.sharding import PartitionSpec as P

CHANNELS = 64
FINE = 512
TAPS = 16
FINE_TAPS = 12


def from_behind(array, axis, by):
    length = lax.axis_size(axis)
    pairs = [(i, i + by) for i in range(length) if 0 <= i + by < length]
    return lax.ppermute(array, axis, pairs)


def tables(points):
    counter = jnp.arange(points, dtype=jnp.int32)
    product = counter[:, None] * counter[None, :] % points
    angle = product.astype(jnp.float32) * (2.0 * math.pi / points)
    return (jnp.cos(angle), jnp.sin(angle))


def coarse_branches(extended, coarse_taps, length):
    row_count = length // (2 * CHANNELS)
    summed = jnp.zeros((2, row_count, 2 * CHANNELS), jnp.float32)
    for tap_index in range(TAPS):
        offset = (TAPS - 1 - tap_index) * CHANNELS
        segment = extended[:, offset : offset + length].reshape(2, row_count, 2 * CHANNELS)
        summed = summed + segment * jnp.tile(coarse_taps[tap_index], 2)
    return summed.reshape(2, length // CHANNELS, CHANNELS)


def coarse_spectrum(branches, cosine_rows, sine_rows):
    factor = 1.0 / math.sqrt(CHANNELS)
    highest = lax.Precision.HIGHEST
    real_part = (
        jnp.einsum("kp,tp->kt", cosine_rows, branches[0], precision=highest)
        + jnp.einsum("kp,tp->kt", sine_rows, branches[1], precision=highest)
    ) * factor
    imag_part = (
        jnp.einsum("kp,tp->kt", cosine_rows, branches[1], precision=highest)
        - jnp.einsum("kp,tp->kt", sine_rows, branches[0], precision=highest)
    ) * factor
    return jnp.stack([real_part, imag_part])


def fine_section(coarse, fine_taps):
    group_size = coarse.shape[1]
    fine_frames = coarse.shape[2] // FINE
    shaped = coarse.reshape(2, group_size, fine_frames, FINE)
    padded = jnp.pad(shaped, ((0, 0), (0, 0), (FINE_TAPS - 1, 0), (0, 0)))
    summed = jnp.zeros((2, group_size, fine_frames, FINE), jnp.float32)
    for tap_index in range(FINE_TAPS):
        offset = FINE_TAPS - 1 - tap_index
        summed = summed + fine_taps[tap_index] * padded[:, :, offset : offset + fine_frames, :]
    cosine_table, sine_table = tables(FINE)
    factor = 1.0 / math.sqrt(FINE)
    highest = lax.Precision.HIGHEST
    out_real = (
        jnp.matmul(summed[0], cosine_table, precision=highest)
        + jnp.matmul(summed[1], sine_table, precision=highest)
    ) * factor
    out_imag = (
        jnp.matmul(summed[1], cosine_table, precision=highest)
        - jnp.matmul(summed[0], sine_table, precision=highest)
    ) * factor
    return jnp.stack([out_real, out_imag])


def on_device(signal, coarse_taps, fine_taps):
    length = signal.shape[1]
    history = (TAPS - 1) * CHANNELS
    cosine_table, sine_table = tables(CHANNELS)
    previous = from_behind(signal[:, length - history :], "tm", 1)
    extended = jnp.concatenate([previous, signal], axis=1)
    branches = coarse_branches(extended, coarse_taps, length)
    coarse = lax.all_to_all(
        coarse_spectrum(branches, cosine_table, sine_table),
        "tm",
        split_axis=1,
        concat_axis=2,
        tiled=True,
    )
    return fine_section(coarse, fine_taps)


def solution(mesh):
    return jax.shard_map(
        on_device,
        mesh=mesh,
        in_specs=(P(None, ("streams", "tm")), P(), P()),
        out_specs=P(None, "tm", "streams", None),
        check_vma=False,
    )
```

profile of v0, /device:TPU:0, one launch (start us, length us, event | category | flops | bytes accessed | tf_op | source)
XLA Modules:
  0.0 54.4 jit_solution(16357406457331470736)
XLA Ops:
  0.0 0.8 %slice.180 = f32[2,960]{1,0:T(2,128)S(1)} slice(f32[2,65536]{1,0:T(2,128)} %param.3), slice={[0:2], [64576:65536]} | slice | bytes 15360 | tf_op jit(solution)/shard_map/slice | solution.py:78
  0.8 2.4 %collective-permute-start = (f32[2,960]{1,0:T(2,128)S(1)}, f32[2,960]{1,0:T(2,128)S(1)}, u32[]{:S(2)}, u32[]{:S(2)}) collective-permute-start(f32[2,960]{1,0:T(2,128)S(1)} %slice.180), channel_id=1, source_target_pairs={{0,1},{1,2},{2,3},{4,5},{5,6},{6,7},{8,9},{9,10},{10,11},{12,13},{... | collective-permute-start | bytes 23048 | tf_op jit(solution)/shard_map/ppermute | solution.py:17
  3.2 1.0 %slice_bitcast_fusion.21 = (f32[64]{0:T(128)S(1)}, f32[64]{0:T(128)S(1)}, f32[64]{0:T(128)S(1)}, f32[64]{0:T(128)S(1)}, f32[64]{0:T(128)S(1)}, /*index=5*/f32[64...) fusion(f32[16,64]{1,0:T(8,128)} %param.4), kind=kLoop, calls=%fused_computation.166 | loop fusion | bytes 8192 | tf_op jit(solution)/shard_map/tile | solution.py:33
  5.6 4.7 %fusion.23 = (f32[1,2,512,128]{3,1,2,0:T(2,128)S(1)}, f32[1,2,512,128]{3,1,2,0:T(2,128)S(1)}, f32[1,2,512,128]{3,1,2,0:T(2,128)S(1)}, f32[1,2,512,128]{3,1,2,0:T...) fusion(f32[2,960]{1,0:T(2,128)S(1)} %collective-permute-done, f32[2,65536]{1,0:T(2,128)} %param.3), kind=kLoop, calls=%fused_computation.51 | loop fusion | flops 786432 | bytes 3677696
  10.3 2.6 %fusion.35 = (f32[1,2,512,128]{3,1,2,0:T(2,128)S(1)}, f32[1,2,512,128]{3,1,2,0:T(2,128)S(1)}, f32[1,2,512,128]{3,1,2,0:T(2,128)S(1)}, f32[1,2,512,128]{3,1,2,0:T...) fusion(f32[2,960]{1,0:T(2,128)S(1)} %collective-permute-done, f32[2,65536]{1,0:T(2,128)S(1)} %copy-done), kind=kLoop, calls=%fused_computation.63 | loop fusion | flops 786432 | bytes 3677696
  12.9 1.3 %fusion.47 = (f32[1,2,512,128]{3,1,2,0:T(2,128)S(1)}, f32[1,2,512,128]{3,1,2,0:T(2,128)S(1)}, f32[1,2,512,128]{3,1,2,0:T(2,128)S(1)}) fusion(f32[2,960]{1,0:T(2,128)S(1)} %collective-permute-done, f32[2,65536]{1,0:T(2,128)S(1)} %copy-done), kind=kLoop, calls=%fused_computation.75 | loop fusion | flops 393216 | bytes 2104832
  14.2 0.6 %fusion.66 = f32[2,512,128]{2,1,0:T(8,128)S(1)} fusion(f32[1,2,512,128]{3,1,2,0:T(2,128)S(1)} %get-tuple-element.18, f32[1,2,512,128]{3,1,2,0:T(2,128)S(1)} %get-tuple-element.19, f32[1,2,512,128]{3,1,2,0:T(2,128)S(1)} %get-tuple-element.17, f32[1,2,512,128]{3,1,2,0:T(2,128)S(1)} %get-tuple-element.16, f32[1,2,512,128]{3,1,2,0:T(2,128)S(1)} %get-tuple-element.15, ...), kind=kLoop, calls=%fused_computation.95 | loop fusion | flops 4063232 | bytes 8921088 | tf_op jit(solution)/shard_map/add | solution.py:33
  14.8 0.1 squeeze.16
  15.0 0.8 %fusion.98 = f32[64,1024]{1,0:T(8,128)S(1)} fusion(f32[1024,64]{1,0:T(8,128)S(1)} %squeeze.16), kind=kOutput, calls=%fused_computation.146 | convolution fusion | flops 50388992 | bytes 524288 | tf_op jit(solution)/shard_map/kp,tp->kt/dot_general | solution.py:41
  15.8 0.2 squeeze.17
  15.9 0.8 %fusion.96 = f32[64,1024]{1,0:T(8,128)S(1)} fusion(f32[1024,64]{1,0:T(8,128)S(1)} %squeeze.17), kind=kOutput, calls=%fused_computation.145 | convolution fusion | flops 50388992 | bytes 524288 | tf_op jit(solution)/shard_map/kp,tp->kt/dot_general | solution.py:45
  16.7 0.8 %fusion.3 = f32[1,64,1024]{2,1,0:T(8,128)S(1)} fusion(f32[64,1024]{1,0:T(8,128)S(1)} %fusion.98, f32[1024,64]{1,0:T(8,128)S(1)} %squeeze.17), kind=kOutput, calls=%fused_computation.29 | convolution fusion | flops 50520064 | bytes 786432 | tf_op jit(solution)/shard_map/kp,tp->kt/dot_general | solution.py:42
  17.5 0.8 %fusion.1 = f32[1,64,1024]{2,1,0:T(8,128)S(1)} fusion(f32[64,1024]{1,0:T(8,128)S(1)} %fusion.96, f32[1024,64]{1,0:T(8,128)S(1)} %squeeze.16), kind=kOutput, calls=%fused_computation.26 | convolution fusion | flops 50520064 | bytes 786432 | tf_op jit(solution)/shard_map/kp,tp->kt/dot_general | solution.py:46
  18.4 1.2 %copy.6 = f32[2,64,1024]{2,0,1:T(2,128)} copy(f32[2,64,1024]{2,1,0:T(8,128)S(1)} %pad_maximum_fusion.1) | data formatting | bytes 1048576 | tf_op jit(solution)/shard_map/stack | solution.py:48
  19.6 4.5 %all-to-all-start = ((f32[2,64,1024]{2,0,1:T(2,128)}), f32[2,64,1024]{2,0,1:T(2,128)S(1)}, u32[]{:S(2)}, u32[]{:S(2)}) async-start(f32[2,64,1024]{2,0,1:T(2,128)} %copy.6), calls=%async_computation | async-start | bytes 1048576 | tf_op jit(solution)/shard_map/all_to_all | solution.py:81
  24.1 8.8 %all-to-all-done = f32[2,64,1024]{2,0,1:T(2,128)S(1)} async-done(((f32[2,64,1024]{2,0,1:T(2,128)}), f32[2,64,1024]{2,0,1:T(2,128)S(1)}, u32[]{:S(2)}, u32[]{:S(2)}) %all-to-all-start) | async-done | bytes 524320 | tf_op jit(solution)/shard_map/all_to_all | solution.py:81
  32.9 0.3 copy.41
  33.3 0.2 reshape.109
  33.5 0.6 %fusion.59 = f32[2,16,8,512]{3,2,1,0:T(8,128)S(1)} fusion(f32[2,16,8,512]{3,2,1,0:T(8,128)S(1)} %reshape.109, f32[512]{0:T(512)S(1)} %bitcast.214, f32[512]{0:T(512)S(1)} %bitcast.215, f32[512]{0:T(512)S(1)} %bitcast.205, f32[512]{0:T(512)S(1)} %bitcast.206, f32[512]{0:T(512)S(1)} %bitcast.207, f32[512]{0:T(512)S(1)} %bitcast.208, f32[512]{0:T(512)S(1)} %bitcast.209, ...), kind=kLoop, calls=%fused_computation.87 | loop fusion | flops 2490368 | bytes 1073152 | tf_op jit(solution)/shard_map/add | solution.py:59
  34.1 4.9 %fusion.15 = f32[16,8,512]{2,1,0:T(8,128)S(1)} fusion(f32[2,16,8,512]{3,2,1,0:T(8,128)S(1)} %fusion.59), kind=kOutput, calls=%fused_computation.43 | convolution fusion | flops 406323200 | bytes 524288 | tf_op jit(solution)/shard_map/dot_general | solution.py:64
  39.0 4.9 %fusion.13 = f32[16,8,512]{2,1,0:T(8,128)S(1)} fusion(f32[2,16,8,512]{3,2,1,0:T(8,128)S(1)} %fusion.59), kind=kOutput, calls=%fused_computation.41 | convolution fusion | flops 406323200 | bytes 524288 | tf_op jit(solution)/shard_map/dot_general | solution.py:68
  43.8 4.9 %fusion.7 = f32[1,16,8,512]{3,2,1,0:T(8,128)S(1)} fusion(f32[16,8,512]{2,1,0:T(8,128)S(1)} %fusion.15, f32[2,16,8,512]{3,2,1,0:T(8,128)S(1)} %fusion.59), kind=kOutput, calls=%fused_computation.35 | convolution fusion | flops 406454272 | bytes 786432 | tf_op jit(solution)/shard_map/dot_general | solution.py:65
  48.7 4.9 %fusion.5 = f32[1,16,8,512]{3,2,1,0:T(8,128)S(1)} fusion(f32[16,8,512]{2,1,0:T(8,128)S(1)} %fusion.13, f32[2,16,8,512]{3,2,1,0:T(8,128)S(1)} %fusion.59), kind=kOutput, calls=%fused_computation.32 | convolution fusion | flops 406454272 | bytes 786432 | tf_op jit(solution)/shard_map/dot_general | solution.py:69
  53.6 0.8 %pad_maximum_fusion.2 = f32[2,16,8,512]{3,2,1,0:T(8,128)} fusion(f32[1,16,8,512]{3,2,1,0:T(8,128)S(1)} %fusion.5, f32[1,16,8,512]{3,2,1,0:T(8,128)S(1)} %fusion.7), kind=kLoop, calls=%fused_computation.128 | loop fusion | flops 131072 | bytes 1048576 | tf_op jit(solution)/shard_map/stack | solution.py:71
  (40 shorter events, 1.5 us)
Async XLA Ops:
  0.8 4.8 %collective-permute-start = (f32[2,960]{1,0:T(2,128)S(1)}, f32[2,960]{1,0:T(2,128)S(1)}, u32[]{:S(2)}, u32[]{:S(2)}) collective-permute-start(f32[2,960]{1,0:T(2,128)S(1)} %slice.180), channel_id=1, source_target_pairs={{0,1},{1,2},{2,3},{4,5},{5,6},{6,7},{8,9},{9,10},{10,11},{12,13},{... | collective-permute-start | bytes 23048 | tf_op jit(solution)/shard_map/ppermute | solution.py:17
  5.6 4.7 %copy-start = (f32[2,65536]{1,0:T(2,128)S(1)}, f32[2,65536]{1,0:T(2,128)}, u32[]{:S(2)}) copy-start(f32[2,65536]{1,0:T(2,128)} %param.3) | copy-start | bytes 1572868
  19.6 4.5 %copy-start.1 = (f32[12,512]{1,0:T(8,128)S(1)}, f32[12,512]{1,0:T(8,128)}, u32[]{:S(2)}) copy-start(f32[12,512]{1,0:T(8,128)} %param.5) | copy-start | bytes 73732
  19.6 13.3 %all-to-all-start = ((f32[2,64,1024]{2,0,1:T(2,128)}), f32[2,64,1024]{2,0,1:T(2,128)S(1)}, u32[]{:S(2)}, u32[]{:S(2)}) async-start(f32[2,64,1024]{2,0,1:T(2,128)} %copy.6), calls=%async_computation | async-start | bytes 1048576 | tf_op jit(solution)/shard_map/all_to_all | solution.py:81
where the time goes:
time: 54.7 us; the launch traced here: 54.4 us
  matrix products  22.7 us (41%)
  other arithmetic  10.6 us (19%)
  waiting for transfers between devices  8.79 us (16%)
  starting transfers between devices  6.89 us (13%)
  local copies, waits for them, and re-layouts  5.27 us (10%)
    all_to_all x1, waiting for transfers between devices, on_device(): lax.all_to_all(coarse_spectrum(branches, cosine_table, sine_table), 'tm',...  8.79 us
    unnamed x3, other arithmetic  8.52 us
    dot_general x1, matrix products, fine_section(): jnp.matmul(summed[0], cosine_table, precision=highest)  4.87 us
    dot_general x1, matrix products, fine_section(): jnp.matmul(summed[1], cosine_table, precision=highest)  4.87 us
    dot_general x1, matrix products, fine_section(): jnp.matmul(summed[0], sine_table, precision=highest)  4.86 us
    dot_general x1, matrix products, fine_section(): jnp.matmul(summed[1], sine_table, precision=highest)  4.86 us
    all_to_all x1, starting transfers between devices, on_device(): lax.all_to_all(coarse_spectrum(branches, cosine_table, sine_table), 'tm',...  4.5 us
    ppermute x1, starting transfers between devices, from_behind(): return lax.ppermute(array, axis, pairs)  2.39 us
  transfers between devices with their start and end apart: 2, of which 1 were waited for; matrix products, arithmetic and copies ran while one was open for 4% of the time, Pallas kernels for 0%

commit v1 on v0

v1 whole, which is shorter than its diff:
```python
import math

import jax
import jax.numpy as jnp
import numpy as np
from jax import lax
from jax.experimental import pallas as pl
from jax.experimental.pallas import tpu as pltpu
from jax.sharding import PartitionSpec as P

LANES = 128
F32, BF16 = jnp.float32, jnp.bfloat16


def split_table(table):
    high = np.asarray(table, np.float32).astype(jnp.bfloat16)
    low = (np.asarray(table, np.float64) - high.astype(np.float64)).astype(np.float32).astype(jnp.bfloat16)
    return high, low


def complex_table(turns, points, factor):
    angle = (turns % points) * (2.0 * math.pi / points)
    return np.cos(angle) * factor, -np.sin(angle) * factor


def coarse_table(channels, groups):
    halves, per = LANES // channels, channels // groups
    k, p = np.arange(channels), np.arange(channels)
    real, imag = complex_table(k[:, None] * p[None, :], channels, 1.0 / math.sqrt(channels))
    table = np.zeros((groups, 2, halves, per, 2, halves, channels))
    real, imag = real.reshape(groups, per, channels), imag.reshape(groups, per, channels)
    for half in range(halves):
        table[:, 0, half, :, 0, half] = real
        table[:, 0, half, :, 1, half] = -imag
        table[:, 1, half, :, 0, half] = imag
        table[:, 1, half, :, 1, half] = real
    return table.reshape(2 * LANES, 2 * LANES)


def fine_tables(fine):
    radix = fine // LANES
    i = np.arange(LANES)
    real, imag = complex_table(i[:, None] * i[None, :], LANES, 1.0 / math.sqrt(fine))
    table = np.block([[real, imag], [-imag, real]])
    real, imag = complex_table(np.arange(radix)[:, None] * i[None, :], fine, 1.0)
    return table, np.stack([real, imag], axis=1).astype(np.float32)


def split_value(value):
    high = value.astype(BF16)
    return high, (value - high.astype(F32)).astype(BF16)


def dot_nt(left, right):
    return lax.dot_general(left, right, (((1,), (1,)), ((), ())), preferred_element_type=F32)


def dot_nn(left, right):
    return lax.dot_general(left, right, (((1,), (0,)), ((), ())), preferred_element_type=F32)


VMEM = pl.BlockSpec(memory_space=pltpu.VMEM)
ANY = pl.BlockSpec(memory_space=pl.ANY)
PARAMS = pltpu.CompilerParams(vmem_limit_bytes=24 * 1024 * 1024)


def in_vmem(value):
    return pltpu.with_memory_space_constraint(value, pltpu.VMEM)


def coarse_kernel(axis, groups, x_hbm, taps_ref, high_ref, low_ref, *rest):
    outs, (xs, ys, bs, sem) = rest[:groups], rest[groups:]
    rows = x_hbm.shape[0]
    channels = taps_ref.shape[1]
    taps_count = taps_ref.shape[0]
    pad = 16
    copy = pltpu.make_async_copy(x_hbm, xs.at[pl.ds(pad, rows)], sem)
    copy.start()
    zeros = jnp.zeros((pad, LANES), F32)
    xs[:pad] = zeros
    xs[pad + rows :] = zeros
    taps = taps_ref[...]
    taps = jnp.concatenate([taps, taps], axis=1)
    me = lax.axis_index(axis)
    span = 2 * LANES // groups
    picks = [pl.multiple_of((me ^ step) * span, span) for step in range(groups)]
    high = jnp.concatenate([high_ref[pl.ds(pick, span), :] for pick in picks], axis=0)
    low = jnp.concatenate([low_ref[pl.ds(pick, span), :] for pick in picks], axis=0)
    copy.wait()

    lane = lax.broadcasted_iota(jnp.int32, (1, LANES), 1)
    lower = lane < channels
    total = rows + pad
    ys[:pad] = zeros
    block = 80
    for base in range(0, total, block):
        now = xs[pad + base : pad + base + block]
        before = xs[pad + base - 2 : pad + base + block - 2]
        ys[pad + base : pad + base + block] = pltpu.roll(jnp.where(lower, now, before), channels, 1)
    for base in range(0, total, block):
        summed = None
        for parity, source in ((0, xs), (1, ys)):
            for shift in range(taps_count // 4):
                start = pad + base - 2 * shift - 8
                piece = source[start : start + block + 8]
                near = taps[2 * shift + parity][None, :]
                far = taps[2 * (shift + 4) + parity][None, :]
                term = piece[8:] * near + piece[:block] * far
                summed = term if summed is None else summed + term
        bs[base : base + block] = summed

    half_rows = rows // 2
    for frame in range(2):
        parts = []
        for a in range(2):
            pair = [bs[pl.ds(frame * half_rows + 2 * a + part, LANES, stride=4), :] for part in range(2)]
            parts.append(jnp.concatenate(pair, axis=1))
        bh, bl = split_value(jnp.concatenate(parts, axis=0))
        result = dot_nt(high, bh) + dot_nt(low, bh) + dot_nt(high, bl)
        for step in range(groups):
            for a in range(2):
                at = (frame * 2 + a) * span
                outs[step][at : at + span] = result[step * span : (step + 1) * span, a * LANES : (a + 1) * LANES]
    parts = []
    for a in range(2):
        pair = [bs[pl.ds(rows + 2 * a + part, 4, stride=4), :] for part in range(2)]
        parts.append(jnp.concatenate(pair, axis=1))
    bh, bl = split_value(jnp.concatenate(parts, axis=0))
    tail = dot_nt(bh, high) + dot_nt(bh, low) + dot_nt(bl, high)
    for step in range(groups):
        at = step * span // LANES * LANES
        outs[step][4 * span : 4 * span + 8] = tail[:, at : at + LANES]


def coarse_section(signal, coarse_taps, axis, groups):
    length = signal.shape[1]
    channels = coarse_taps.shape[1]
    chunks = length // LANES
    rows = signal.reshape(2, chunks, LANES).transpose(1, 0, 2).reshape(2 * chunks, LANES)
    high, low = split_table(coarse_table(channels, groups))
    span = 2 * LANES // groups
    kernel = lambda *refs: coarse_kernel(axis, groups, *refs)
    return pl.pallas_call(
        kernel,
        out_shape=[pltpu.VMEM((4 * span + 8, LANES), F32)] * groups,
        in_specs=[ANY, VMEM, VMEM, VMEM],
        out_specs=[VMEM] * groups,
        scratch_shapes=[
            pltpu.VMEM((2 * chunks + 32, LANES), F32),
            pltpu.VMEM((2 * chunks + 32, LANES), F32),
            pltpu.VMEM((2 * chunks + 16, LANES), F32),
            pltpu.SemaphoreType.DMA,
        ],
        compiler_params=PARAMS,
        name="coarse",
    )(rows, coarse_taps, jnp.asarray(high), jnp.asarray(low))


def fine_kernel(axis, groups, taps_ref, high_ref, low_ref, turn_ref, *rest):
    pieces, out_ref, (xs, yh, yl, zs) = rest[:groups], rest[groups], rest[groups + 1 :]
    span = 2 * LANES // groups
    per = span // 4
    frames = 2 * groups
    taps_count = taps_ref.shape[1]
    me = lax.axis_index(axis)
    for step in range(groups):
        owner = me ^ step
        for frame in range(2):
            for a in range(2):
                at = (frame * 2 + a) * span
                xs[2 * owner + frame, a] = pieces[step][at : at + span]
    lane = lax.broadcasted_iota(jnp.int32, (1, LANES), 1)
    for step in range(groups):
        owner = me ^ step
        tail = jnp.transpose(pieces[step][4 * span : 4 * span + 8])
        at = step * span % LANES
        tail = tail[at : at + span]
        for a in range(2):
            into = xs[2 * owner + 2, a, :, 0:4]
            xs[2 * owner + 2, a, :, 0:4] = into + tail[:, 4 * a : 4 * a + 4]
    for a in range(2):
        for h in range(2):
            phase = 2 * a + h
            for part in range(2):
                at = (2 * part + h) * per
                for m in range(frames):
                    summed = None
                    for j in range(min(m + 1, taps_count)):
                        term = xs[m - j, a, at : at + per] * taps_ref[phase, j : j + 1]
                        summed = term if summed is None else summed + term
                    high, low = split_value(summed)
                    yh[phase, m * per : (m + 1) * per, part * LANES : (part + 1) * LANES] = high
                    yl[phase, m * per : (m + 1) * per, part * LANES : (part + 1) * LANES] = low
    height = 4 * frames * per
    left, right = yh[...].reshape(height, 2 * LANES), yl[...].reshape(height, 2 * LANES)
    high, low = high_ref[...], low_ref[...]
    zs[...] = (dot_nn(left, high) + dot_nn(right, high) + dot_nn(left, low)).reshape(4, frames * per, 2 * LANES)
    size = min(8, per)
    blocks = frames // 8
    for at in range(0, frames * per, 8):
        z = []
        for phase in range(4):
            real, imag = zs[phase, at : at + 8, :LANES], zs[phase, at : at + 8, LANES:]
            if phase:
                c, s = turn_ref[phase, 0:1], turn_ref[phase, 1:2]
                real, imag = real * c - imag * s, real * s + imag * c
            z.append((real, imag))
        (ar, ai), (br, bi), (cr, ci), (dr, di) = z
        pr, pi, qr, qi = ar + cr, ai + ci, ar - cr, ai - ci
        ur, ui, vr, vi = br + dr, bi + di, br - dr, bi - di
        reals = (pr + ur, qr + vi, pr - ur, qr - vi)
        imags = (pi + ui, qi - vr, pi - ui, qi + vr)
        for part, values in enumerate((reals, imags)):
            for r, value in enumerate(values):
                for inner in range(0, 8, size):
                    m, k = divmod(at + inner, per)
                    row = (((part * per + k) * blocks + m // 8) * 4 + r) * 8 + m % 8
                    out_ref[pl.ds(row, size, stride=32 * blocks), :] = value[inner : inner + size]


def fine_section(pieces, fine_taps, axis, groups):
    fine = fine_taps.shape[1]
    taps_count = fine_taps.shape[0]
    span = 2 * LANES // groups
    per, frames = span // 4, 2 * groups
    taps = fine_taps.reshape(taps_count, LANES, fine // LANES).transpose(2, 0, 1)
    table, turns = fine_tables(fine)
    high, low = split_table(table)
    kernel = lambda *refs: fine_kernel(axis, groups, *refs)
    out = pl.pallas_call(
        kernel,
        out_shape=jax.ShapeDtypeStruct((2 * per * frames * 4, LANES), F32),
        in_specs=[VMEM] * (4 + groups),
        out_specs=VMEM,
        scratch_shapes=[
            pltpu.VMEM((frames + 2, 2, span, LANES), F32),
            pltpu.VMEM((4, frames * per, 2 * LANES), BF16),
            pltpu.VMEM((4, frames * per, 2 * LANES), BF16),
            pltpu.VMEM((4, frames * per, 2 * LANES), F32),
        ],
        compiler_params=PARAMS,
        name="fine",
    )(taps, jnp.asarray(high), jnp.asarray(low), jnp.asarray(turns), *[in_vmem(piece) for piece in pieces])
    out = out.reshape(2, per, frames // 8, 4, 8, LANES).transpose(0, 1, 2, 4, 3, 5)
    return out.reshape(2, per, frames, 4 * LANES)


def solution(mesh):
    axis = "tm"
    groups = mesh.shape[axis]

    def on_device(signal, coarse_taps, fine_taps):
        pieces = coarse_section(signal, coarse_taps, axis, groups)
        moved = [pieces[0]]
        for step in range(1, groups):
            moved.append(lax.ppermute(pieces[step], axis, [(i, i ^ step) for i in range(groups)]))
        return fine_section(moved, fine_taps, axis, groups)

    return jax.shard_map(
        on_device,
        mesh=mesh,
        in_specs=(P(None, ("streams", "tm")), P(), P()),
        out_specs=P(None, "tm", "streams", None),
        check_vma=False,
    )
```

time: 54.7 us -> 16.7 us (0.31)
  matrix products: 22.7 us -> 0 us
  other arithmetic: 10.6 us -> 0 us
  starting transfers between devices: 6.89 us -> 3.18 us
  Pallas kernels: 0 us -> 2.91 us
  waiting for transfers between devices: 8.79 us -> 6.48 us
  local copies, waits for them, and re-layouts: 5.27 us -> 3.81 us
    dot_general x8 -> x0, matrix products: 22.7 us -> none  [the longest x1 4.87 us: fine_section(): jnp.matmul(summed[0], cosine_table, precision=highest)]
    all_to_all x1 -> x0, waiting for transfers between devices: 8.79 us -> none  [on_device(): lax.all_to_all(coarse_spectrum(branches, cosine_table, sine_table), 'tm',...]
    unnamed x3 -> x0, other arithmetic: 8.52 us -> none
    ppermute x1 -> x3, waiting for transfers between devices: 0.01 us -> 6.48 us  [on_device(): lax.ppermute(pieces[step], axis, [(i, i ^ step) for i in range(groups)])]
    all_to_all x1 -> x0, starting transfers between devices: 4.5 us -> none  [on_device(): lax.all_to_all(coarse_spectrum(branches, cosine_table, sine_table), 'tm',...]
    unnamed x4 -> x17, local copies, waits for them, and re-layouts: 0.01 us -> 3.71 us
    pallas_call x0 -> x2, Pallas kernels: none -> 2.91 us  [the longest x1 1.77 us: fine_section(): pl.pallas_call(kernel, out_shape=jax.ShapeDtypeStruct((2 * per * frames *...]
    another operation x18 -> x0, local copies, waits for them, and re-layouts: 2.26 us -> none  [the longest x1 1.2 us: coarse_spectrum(): return jnp.stack([real_part, imag_part])]
  transfers between devices with their start and end apart: 2 -> 3, of which waited for: 1 -> 2; matrix products, arithmetic and copies ran while one was open for 4% -> 1% of each run, Pallas kernels for 0% -> 0%
where the time goes in v1:
time: 16.7 us; the launch traced here: 16.4 us
  waiting for transfers between devices  6.48 us (39%)
  local copies, waits for them, and re-layouts  3.81 us (23%)
  starting transfers between devices  3.18 us (19%)
  Pallas kernels  2.91 us (17%)
    ppermute x3, waiting for transfers between devices, on_device(): lax.ppermute(pieces[step], axis, [(i, i ^ step) for i in range(groups)])  6.48 us
    unnamed x17, local copies, waits for them, and re-layouts  3.71 us
    ppermute x3, starting transfers between devices, on_device(): lax.ppermute(pieces[step], axis, [(i, i ^ step) for i in range(groups)])  3.18 us
    pallas_call x1, Pallas kernels, fine_section(): pl.pallas_call(kernel, out_shape=jax.ShapeDtypeStruct((2 * per * frames *...  1.77 us
    pallas_call x1, Pallas kernels, coarse_section(): pl.pallas_call(kernel, out_shape=[pltpu.VMEM((4 * span + 8, LANES), F32)]...  1.13 us
  transfers between devices with their start and end apart: 3, of which 2 were waited for; matrix products, arithmetic and copies ran while one was open for 1% of the time, Pallas kernels for 0%

profile of v1, /device:TPU:0, one launch (start us, length us, event | category | flops | bytes accessed | tf_op | source)
XLA Modules:
  0.0 16.4 jit_solution(16134702450141926301)
XLA Ops:
  0.0 0.0 copy-start
  0.0 1.0 %copy-done = f32[2,65536]{1,0:T(2,128)S(1)} copy-done((f32[2,65536]{1,0:T(2,128)S(1)}, f32[2,65536]{1,0:T(2,128)}, u32[]{:S(2)}) %copy-start) | copy-done | bytes 524312
  1.0 0.0 copy-start.1
  1.0 0.9 %copy-done.1 = bf16[256,256]{1,0:T(8,128)(2,1)S(1)} copy-done((bf16[256,256]{1,0:T(8,128)(2,1)S(1)}, bf16[256,256]{1,0:T(8,128)(2,1)}, u32[]{:S(2)}) %copy-start.1) | copy-done | bytes 131096
  1.9 0.0 copy-start.2
  1.9 0.9 %copy-done.2 = bf16[256,256]{1,0:T(8,128)(2,1)S(1)} copy-done((bf16[256,256]{1,0:T(8,128)(2,1)S(1)}, bf16[256,256]{1,0:T(8,128)(2,1)}, u32[]{:S(2)}) %copy-start.2) | copy-done | bytes 131096
  2.9 0.7 %copy-done.5 = f32[16,64]{1,0:T(8,128)S(1)} copy-done((f32[16,64]{1,0:T(8,128)S(1)}, f32[16,64]{1,0:T(8,128)}, u32[]{:S(2)}) %copy-start.5) | copy-done | bytes 4120
  3.6 1.1 %coarse.1 = (f32[264,128]{1,0:T(8,128)S(1)}, f32[264,128]{1,0:T(8,128)S(1)}, f32[264,128]{1,0:T(8,128)S(1)}, f32[264,128]{1,0:T(8,128)S(1)}) custom-call(f32[1024,128]{1,0:T(8,128)S(1)} %bitcast.12, f32[16,64]{1,0:T(8,128)S(1)} %copy-done.5, bf16[256,256]{1,0:T(8,128)(2,1)S(1)} %copy-done.2, bf16[256,256]{1,0:T(8,128)(2,1)S(1)} %copy-done.1), custom_call_target="tpu_custom_call" | custom-call | tf_op jit(solution)/shard_map/coarse/pallas_call | solution.py:143
  4.7 0.6 %collective-permute-start = (f32[264,128]{1,0:T(8,128)S(1)}, f32[264,128]{1,0:T(8,128)S(1)}, u32[]{:S(2)}, u32[]{:S(2)}) collective-permute-start(f32[264,128]{1,0:T(8,128)S(1)} %get-tuple-element.10), channel_id=1, source_target_pairs={{0,1},{1,0},{2,3},{3,2},{4,5},{5,4},{6,7},{7,6},{8,9},{9,8},{10,11... | collective-permute-start | bytes 405512 | tf_op jit(solution)/shard_map/ppermute | solution.py:256
  5.2 2.6 %collective-permute-start.1 = (f32[264,128]{1,0:T(8,128)S(1)}, f32[264,128]{1,0:T(8,128)S(1)}, u32[]{:S(2)}, u32[]{:S(2)}) collective-permute-start(f32[264,128]{1,0:T(8,128)S(1)} %get-tuple-element.11), channel_id=1, source_target_pairs={{0,2},{1,3},{2,0},{3,1},{4,6},{5,7},{6,4},{7,5},{8,10},{9,11},{10,... | collective-permute-start | bytes 405512 | tf_op jit(solution)/shard_map/ppermute | solution.py:256
  7.8 0.0 collective-permute-start.2
  7.9 0.0 copy-done.7
  7.9 0.1 copy.10
  8.0 0.0 copy-start.3
  8.0 0.0 copy-start.4
  8.0 0.0 copy-start.6
  8.1 0.1 copy.11
  8.2 0.0 collective-permute-done.refs_5_
  8.2 4.1 %collective-permute-done.1.refs_6_ = f32[264,128]{1,0:T(8,128)S(1)} collective-permute-done((f32[264,128]{1,0:T(8,128)S(1)}, f32[264,128]{1,0:T(8,128)S(1)}, u32[]{:S(2)}, u32[]{:S(2)}) %collective-permute-start.1) | collective-permute-done | bytes 135200 | tf_op jit(solution)/shard_map/ppermute | solution.py:256
  12.3 2.4 %collective-permute-done.2.refs_7_ = f32[264,128]{1,0:T(8,128)S(1)} collective-permute-done((f32[264,128]{1,0:T(8,128)S(1)}, f32[264,128]{1,0:T(8,128)S(1)}, u32[]{:S(2)}, u32[]{:S(2)}) %collective-permute-start.2) | collective-permute-done | bytes 135200 | tf_op jit(solution)/shard_map/ppermute | solution.py:256
  14.6 0.0 copy-done.3
  14.6 0.0 copy-done.4
  14.6 0.0 copy-done.6
  14.7 1.8 %fine.1 = f32[1024,128]{1,0:T(8,128)} custom-call(f32[4,12,128]{2,1,0:T(8,128)S(1)} %bitcast.13, bf16[256,256]{1,0:T(8,128)(2,1)S(1)} %copy-done.4, bf16[256,256]{1,0:T(8,128)(2,1)S(1)} %copy-done.3, f32[4,2,128]{2,1,0:T(2,128)S(1)} %copy-done.6, f32[264,128]{1,0:T(8,128)S(1)} %get-tuple-element.9.refs_4_, f32[264,128]{1,0:T(8,128)S(1)} %collective-permute-done.refs_5_, ...), custom_call_target="tpu_custom_call" | custom-call | tf_op jit(solution)/shard_map/fine/pallas_call | solution.py:230
  (2 shorter events, 0.0 us)
Async XLA Ops:
  0.0 1.0 %copy-start = (f32[2,65536]{1,0:T(2,128)S(1)}, f32[2,65536]{1,0:T(2,128)}, u32[]{:S(2)}) copy-start(f32[2,65536]{1,0:T(2,128)} %param.8) | copy-start | bytes 1572868
  1.0 0.9 %copy-start.1 = (bf16[256,256]{1,0:T(8,128)(2,1)S(1)}, bf16[256,256]{1,0:T(8,128)(2,1)}, u32[]{:S(2)}) copy-start(bf16[256,256]{1,0:T(8,128)(2,1)} %constant.11.clone.refs_3_) | copy-start | bytes 393220
  1.9 0.9 %copy-start.2 = (bf16[256,256]{1,0:T(8,128)(2,1)S(1)}, bf16[256,256]{1,0:T(8,128)(2,1)}, u32[]{:S(2)}) copy-start(bf16[256,256]{1,0:T(8,128)(2,1)} %constant.10.clone.refs_2_) | copy-start | bytes 393220
  2.9 0.7 %copy-start.5 = (f32[16,64]{1,0:T(8,128)S(1)}, f32[16,64]{1,0:T(8,128)}, u32[]{:S(2)}) copy-start(f32[16,64]{1,0:T(8,128)} %refs_1_.2) | copy-start | bytes 12292
  3.5 4.3 %copy-start.7 = (f32[12,512]{1,0:T(8,128)S(1)}, f32[12,512]{1,0:T(8,128)}, u32[]{:S(2)}) copy-start(f32[12,512]{1,0:T(8,128)} %param.10) | copy-start | bytes 73732
  4.7 3.5 %collective-permute-start = (f32[264,128]{1,0:T(8,128)S(1)}, f32[264,128]{1,0:T(8,128)S(1)}, u32[]{:S(2)}, u32[]{:S(2)}) collective-permute-start(f32[264,128]{1,0:T(8,128)S(1)} %get-tuple-element.10), channel_id=1, source_target_pairs={{0,1},{1,0},{2,3},{3,2},{4,5},{5,4},{6,7},{7,6},{8,9},{9,8},{10,11... | collective-permute-start | bytes 405512 | tf_op jit(solution)/shard_map/ppermute | solution.py:256
  5.2 7.0 %collective-permute-start.1 = (f32[264,128]{1,0:T(8,128)S(1)}, f32[264,128]{1,0:T(8,128)S(1)}, u32[]{:S(2)}, u32[]{:S(2)}) collective-permute-start(f32[264,128]{1,0:T(8,128)S(1)} %get-tuple-element.11), channel_id=1, source_target_pairs={{0,2},{1,3},{2,0},{3,1},{4,6},{5,7},{6,4},{7,5},{8,10},{9,11},{10,... | collective-permute-start | bytes 405512 | tf_op jit(solution)/shard_map/ppermute | solution.py:256
  7.8 6.8 %collective-permute-start.2 = (f32[264,128]{1,0:T(8,128)S(1)}, f32[264,128]{1,0:T(8,128)S(1)}, u32[]{:S(2)}, u32[]{:S(2)}) collective-permute-start(f32[264,128]{1,0:T(8,128)S(1)} %get-tuple-element.12), channel_id=1, source_target_pairs={{0,3},{1,2},{2,1},{3,0},{4,7},{5,6},{6,5},{7,4},{8,11},{9,10},{10,... | collective-permute-start | bytes 405512 | tf_op jit(solution)/shard_map/ppermute | solution.py:256
  8.0 6.6 %copy-start.3 = (bf16[256,256]{1,0:T(8,128)(2,1)S(1)}, bf16[256,256]{1,0:T(8,128)(2,1)}, u32[]{:S(2)}) copy-start(bf16[256,256]{1,0:T(8,128)(2,1)} %constant.13.clone.refs_2_) | copy-start | bytes 393220
  8.0 6.6 %copy-start.4 = (bf16[256,256]{1,0:T(8,128)(2,1)S(1)}, bf16[256,256]{1,0:T(8,128)(2,1)}, u32[]{:S(2)}) copy-start(bf16[256,256]{1,0:T(8,128)(2,1)} %constant.12.clone.refs_1_) | copy-start | bytes 393220
  8.0 6.6 %copy-start.6 = (f32[4,2,128]{2,1,0:T(2,128)S(1)}, f32[4,2,128]{2,1,0:T(2,128)}, u32[]{:S(2)}) copy-start(f32[4,2,128]{2,1,0:T(2,128)} %constant.14.clone.refs_3_) | copy-start | bytes 12292

commit v2 on v1

v2 whole, which is shorter than its diff:
```python
import math

import jax
import jax.numpy as jnp
import numpy as np
from jax import lax
from jax.experimental import pallas as pl
from jax.experimental.pallas import tpu as pltpu
from jax.sharding import PartitionSpec as P

LANES = 128
F32, BF16 = jnp.float32, jnp.bfloat16


def split_table(table):
    high = np.asarray(table, np.float32).astype(jnp.bfloat16)
    low = (np.asarray(table, np.float64) - high.astype(np.float64)).astype(np.float32).astype(jnp.bfloat16)
    return high, low


def complex_table(turns, points, factor):
    angle = (turns % points) * (2.0 * math.pi / points)
    return np.cos(angle) * factor, -np.sin(angle) * factor


def coarse_table(channels, groups, chunks):
    halves, per = LANES // channels, channels // (groups * chunks)
    k, p = np.arange(channels), np.arange(channels)
    real, imag = complex_table(k[:, None] * p[None, :], channels, 1.0 / math.sqrt(channels))
    table = np.zeros((groups * chunks, 2, halves, per, 2, halves, channels))
    real, imag = real.reshape(-1, per, channels), imag.reshape(-1, per, channels)
    for half in range(halves):
        table[:, 0, half, :, 0, half] = real
        table[:, 0, half, :, 1, half] = -imag
        table[:, 1, half, :, 0, half] = imag
        table[:, 1, half, :, 1, half] = real
    return table.reshape(2 * LANES, 2 * LANES)


def fine_tables(fine):
    radix = fine // LANES
    i = np.arange(LANES)
    real, imag = complex_table(i[:, None] * i[None, :], LANES, 1.0 / math.sqrt(fine))
    table = np.block([[real, imag], [-imag, real]])
    real, imag = complex_table(np.arange(radix)[:, None] * i[None, :], fine, 1.0)
    return table, np.stack([real, imag], axis=1).astype(np.float32)


def split_value(value):
    high = value.astype(BF16)
    return high, (value - high.astype(F32)).astype(BF16)


def dot_nt(left, right):
    return lax.dot_general(left, right, (((1,), (1,)), ((), ())), preferred_element_type=F32)


def dot_nn(left, right):
    return lax.dot_general(left, right, (((1,), (0,)), ((), ())), preferred_element_type=F32)


VMEM = pl.BlockSpec(memory_space=pltpu.VMEM)
ANY = pl.BlockSpec(memory_space=pl.ANY)
PARAMS = pltpu.CompilerParams(vmem_limit_bytes=24 * 1024 * 1024)


def in_vmem(value):
    return pltpu.with_memory_space_constraint(value, pltpu.VMEM)


PAD = 16
PIECES = 4
TAIL = 16


def in_hbm(value):
    return pltpu.with_memory_space_constraint(value, pltpu.HBM)


def pick_rows(table_ref, half, axis, groups, chunks, chunk):
    me = lax.axis_index(axis)
    span = 2 * LANES // (groups * chunks)
    picks = [pl.multiple_of(((me ^ step) * chunks + chunk) * span, span) for step in range(groups)]
    return jnp.concatenate([table_ref[half, pl.ds(pick, span), :] for pick in picks], axis=0)


def send_chunk(axis, groups, chunks, chunk, table_ref, bh_ref, bl_ref, outs):
    span = 2 * LANES // (groups * chunks)
    high = pick_rows(table_ref, 0, axis, groups, chunks, chunk)
    low = pick_rows(table_ref, 1, axis, groups, chunks, chunk)
    both = jnp.concatenate([high, low], axis=0)
    height = high.shape[0]
    for frame in range(2):
        rows = slice(frame * 2 * LANES, (frame + 1) * 2 * LANES)
        first = dot_nt(both, bh_ref[rows])
        result = first[:height] + first[height:] + dot_nt(high, bl_ref[rows])
        for step in range(groups):
            for a in range(2):
                at = (frame * 2 + a) * span
                outs[step][at : at + span] = result[step * span : (step + 1) * span, a * LANES : (a + 1) * LANES]
    bh, bl = bh_ref[4 * LANES :], bl_ref[4 * LANES :]
    tail = dot_nt(bh, high) + dot_nt(bh, low) + dot_nt(bl, high)
    for step in range(groups):
        at = step * span // LANES * LANES
        outs[step][4 * span : 4 * span + 8] = tail[:8, at : at + LANES]


def coarse_kernel(axis, groups, chunks, x_hbm, taps_hbm, table_hbm, *rest):
    outs, (table_ref, bh_ref, bl_ref, taps_ref, xs, ys, bs, sems) = rest[:groups], rest[groups:]
    rows = x_hbm.shape[0]
    taps_count, channels = taps_hbm.shape
    step = rows // PIECES
    loads = [
        pltpu.make_async_copy(x_hbm.at[pl.ds(i * step, step)], xs.at[pl.ds(PAD + i * step, step)], sems.at[i])
        for i in range(PIECES)
    ]
    get_taps = pltpu.make_async_copy(taps_hbm, taps_ref, sems.at[PIECES])
    get_table = pltpu.make_async_copy(table_hbm, table_ref, sems.at[PIECES + 1])
    get_taps.start()
    for load in loads:
        load.start()
    get_table.start()
    zeros = jnp.zeros((PAD, LANES), F32)
    xs[:PAD] = zeros
    xs[PAD + rows :] = zeros
    ys[:PAD] = zeros
    lane = lax.broadcasted_iota(jnp.int32, (1, LANES), 1)
    lower = lane < channels
    get_taps.wait()
    taps = taps_ref[...]
    taps = jnp.concatenate([taps, taps], axis=1)

    def filtered(base, block):
        now = xs[PAD + base : PAD + base + block]
        before = xs[PAD + base - 2 : PAD + base + block - 2]
        ys[PAD + base : PAD + base + block] = pltpu.roll(jnp.where(lower, now, before), channels, 1)
        summed = None
        for parity, source in ((0, xs), (1, ys)):
            for shift in range(taps_count // 4):
                start = PAD + base - 2 * shift - 8
                piece = source[start : start + block + 8]
                near = taps[2 * shift + parity][None, :]
                far = taps[2 * (shift + 4) + parity][None, :]
                term = piece[8:] * near + piece[:block] * far
                summed = term if summed is None else summed + term
        bs[base : base + block] = summed

    def gathered(base, count, at):
        for a in range(2):
            pair = [bs[pl.ds(base + 2 * a + part, count, stride=4), :] for part in range(2)]
            high, low = split_value(jnp.concatenate(pair, axis=1))
            bh_ref[at + a * count : at + (a + 1) * count] = high
            bl_ref[at + a * count : at + (a + 1) * count] = low

    block = 64
    for i, load in enumerate(loads):
        load.wait()
        for base in range(i * step, (i + 1) * step, block):
            filtered(base, block)
        if i % 2:
            gathered(i // 2 * rows // 2, LANES, i // 2 * 2 * LANES)
    filtered(rows, TAIL)
    pairs = [
        jnp.concatenate([bs[pl.ds(rows + 2 * a + part, 4, stride=4), :] for part in range(2)], axis=1)
        for a in range(2)
    ]
    ending = jnp.concatenate(pairs + [jnp.zeros((8, 2 * LANES), F32)], axis=0)
    bh_ref[4 * LANES :], bl_ref[4 * LANES :] = split_value(ending)
    get_table.wait()
    send_chunk(axis, groups, chunks, 0, table_ref, bh_ref, bl_ref, outs)


def coarse_rest_kernel(axis, groups, chunks, chunk, table_ref, bh_ref, bl_ref, *outs):
    send_chunk(axis, groups, chunks, chunk, table_ref, bh_ref, bl_ref, outs)


def coarse_section(signal, coarse_taps, axis, groups, chunks):
    length = signal.shape[1]
    taps_count, channels = coarse_taps.shape
    count = length // LANES
    rows = signal.reshape(2, count, LANES).transpose(1, 0, 2).reshape(2 * count, LANES)
    table = jnp.asarray(np.stack(split_table(coarse_table(channels, groups, chunks))))
    span = 2 * LANES // (groups * chunks)
    height = 4 * LANES + 16
    message = [pltpu.VMEM((4 * span + 8, LANES), F32)] * groups
    first = pl.pallas_call(
        lambda *refs: coarse_kernel(axis, groups, chunks, *refs),
        out_shape=message
        + [pltpu.VMEM((2, 2 * LANES, 2 * LANES), BF16)]
        + [pltpu.VMEM((height, 2 * LANES), BF16)] * 2,
        in_specs=[ANY, ANY, ANY],
        out_specs=[VMEM] * (groups + 3),
        scratch_shapes=[
            pltpu.VMEM((taps_count, channels), F32),
            pltpu.VMEM((2 * count + 2 * PAD, LANES), F32),
            pltpu.VMEM((2 * count + 2 * PAD, LANES), F32),
            pltpu.VMEM((2 * count + PAD, LANES), F32),
            pltpu.SemaphoreType.DMA((PIECES + 2,)),
        ],
        compiler_params=PARAMS,
        cost_estimate=pl.CostEstimate(flops=2000000, bytes_accessed=1000000, transcendentals=0),
        name="coarse",
    )(in_hbm(rows), in_hbm(coarse_taps), in_hbm(table))
    messages, held = [first[:groups]], [in_vmem(value) for value in first[groups:]]
    for chunk in range(1, chunks):
        more = pl.pallas_call(
            lambda *refs: coarse_rest_kernel(axis, groups, chunks, chunk, *refs),
            out_shape=message,
            in_specs=[VMEM] * 3,
            out_specs=[VMEM] * groups,
            compiler_params=PARAMS,
            cost_estimate=pl.CostEstimate(flops=2000000, bytes_accessed=1000000, transcendentals=0),
            name="coarse_rest",
        )(*held)
        messages.append(more)
    return messages


def fine_kernel(axis, groups, chunks, chunk, *refs):
    taps_ref, high_ref, low_ref, turn_ref = refs[:4]
    pieces = refs[4 : 4 + groups]
    out_hbm, xs, yh, yl, zs, os, sem = refs[-7:]
    span = 2 * LANES // (groups * chunks)
    per = span // 4
    frames = 2 * groups
    taps_count = taps_ref.shape[1]
    me = lax.axis_index(axis)
    for step in range(groups):
        owner = me ^ step
        for frame in range(2):
            for a in range(2):
                at = (frame * 2 + a) * span
                xs[2 * owner + frame, a] = pieces[step][at : at + span]
    for step in range(groups):
        owner = me ^ step
        tail = jnp.transpose(pieces[step][4 * span : 4 * span + 8])
        at = step * span % LANES
        tail = tail[at : at + span]
        for a in range(2):
            into = xs[2 * owner + 2, a, :, 0:4]
            xs[2 * owner + 2, a, :, 0:4] = into + tail[:, 4 * a : 4 * a + 4]
    height = frames * per
    for a in range(2):
        for h in range(2):
            phase = 2 * a + h
            taps = [taps_ref[phase, j : j + 1] for j in range(min(frames, taps_count))]
            sums = []
            for part in range(2):
                at = (2 * part + h) * per
                x = [xs[m, a, at : at + per] for m in range(frames)]
                sums.append([sum((x[m - j] * taps[j] for j in range(1, min(m + 1, taps_count))), x[m] * taps[0]) for m in range(frames)])
            if per % 8 == 0:
                joined = [jnp.concatenate(values, axis=0) for values in sums]
                high, low = split_value(jnp.concatenate(joined, axis=1))
                yh[phase * height : (phase + 1) * height] = high
                yl[phase * height : (phase + 1) * height] = low
            else:
                for part in range(2):
                    for m in range(frames):
                        high, low = split_value(sums[part][m])
                        at = phase * height + m * per
                        yh[at : at + per, part * LANES : (part + 1) * LANES] = high
                        yl[at : at + per, part * LANES : (part + 1) * LANES] = low
    high, low = high_ref[...], low_ref[...]
    zs[...] = dot_nn(yh[...], high) + dot_nn(yl[...], high) + dot_nn(yh[...], low)
    size = min(8, per)
    blocks = frames // 8
    for at in range(0, height, 8):
        z = []
        for phase in range(4):
            row = phase * height + at
            real, imag = zs[row : row + 8, :LANES], zs[row : row + 8, LANES:]
            if phase:
                c, s = turn_ref[phase, 0:1], turn_ref[phase, 1:2]
                real, imag = real * c - imag * s, real * s + imag * c
            z.append((real, imag))
        (ar, ai), (br, bi), (cr, ci), (dr, di) = z
        pr, pi, qr, qi = ar + cr, ai + ci, ar - cr, ai - ci
        ur, ui, vr, vi = br + dr, bi + di, br - dr, bi - di
        reals = (pr + ur, qr + vi, pr - ur, qr - vi)
        imags = (pi + ui, qi - vr, pi - ui, qi + vr)
        for part, values in enumerate((reals, imags)):
            for r, value in enumerate(values):
                for inner in range(0, 8, size):
                    m, k = divmod(at + inner, per)
                    row = ((k * blocks + m // 8) * 4 + r) * 8 + m % 8
                    os[part, pl.ds(row, size, stride=32 * blocks), :] = value[inner : inner + size]
    length = per * blocks * 32
    copies = [
        pltpu.make_async_copy(os.at[part], out_hbm.at[part, pl.ds(chunk * length, length)], sem.at[part])
        for part in range(2)
    ]
    for copy in copies:
        copy.start()
    for copy in copies:
        copy.wait()


def fine_section(moved, fine_taps, axis, groups, chunks):
    taps_count, fine = fine_taps.shape
    span = 2 * LANES // (groups * chunks)
    per, frames = span // 4, 2 * groups
    taps = fine_taps.reshape(taps_count, LANES, fine // LANES).transpose(2, 0, 1)
    table, turns = fine_tables(fine)
    high, low = split_table(table)
    shared = [taps, jnp.asarray(high), jnp.asarray(low), jnp.asarray(turns)]
    height = 4 * frames * per
    length = per * frames * 4
    out = None
    for chunk in range(chunks):
        more = [] if out is None else [out]
        out = pl.pallas_call(
            lambda *refs: fine_kernel(axis, groups, chunks, chunk, *refs),
            out_shape=pltpu.HBM((2, chunks * length, LANES), F32),
            in_specs=[VMEM] * (4 + groups) + [ANY] * len(more),
            out_specs=ANY,
            scratch_shapes=[
                pltpu.VMEM((frames + 2, 2, span, LANES), F32),
                pltpu.VMEM((height, 2 * LANES), BF16),
                pltpu.VMEM((height, 2 * LANES), BF16),
                pltpu.VMEM((height, 2 * LANES), F32),
                pltpu.VMEM((2, length, LANES), F32),
                pltpu.SemaphoreType.DMA((2,)),
            ],
            input_output_aliases={4 + groups: 0} if more else {},
            compiler_params=PARAMS,
            cost_estimate=pl.CostEstimate(flops=2000000, bytes_accessed=1000000, transcendentals=0),
            name="fine",
        )(*[in_vmem(value) for value in shared + list(moved[chunk])], *more)
    out = out.reshape(2, chunks * per, frames // 8, 4, 8, LANES).transpose(0, 1, 2, 4, 3, 5)
    return out.reshape(2, chunks * per, frames, 4 * LANES)


def solution(mesh):
    axis = "tm"
    groups = mesh.shape[axis]

    def on_device(signal, coarse_taps, fine_taps):
        chunks = max(1, coarse_taps.shape[1] // (groups * 8))
        messages = coarse_section(signal, coarse_taps, axis, groups, chunks)
        moved = []
        for message in messages:
            arrived = {0: message[0]}
            for step in range(groups - 1, 0, -1):
                arrived[step] = lax.ppermute(message[step], axis, [(i, i ^ step) for i in range(groups)])
            moved.append([arrived[step] for step in range(groups)])
        return fine_section(moved, fine_taps, axis, groups, chunks)

    return jax.shard_map(
        on_device,
        mesh=mesh,
        in_specs=(P(None, ("streams", "tm")), P(), P()),
        out_specs=P(None, "tm", "streams", None),
        check_vma=False,
    )
```

time: 16.7 us -> 13.8 us (0.83)
  local copies, waits for them, and re-layouts: 3.81 us -> 0.26 us
  waiting for transfers between devices: 6.48 us -> 2.94 us
  starting transfers between devices: 3.18 us -> 5.33 us
  Pallas kernels: 2.91 us -> 5.04 us
    unnamed x17 -> x9, local copies, waits for them, and re-layouts: 3.71 us -> 0.16 us
    ppermute x3 -> x6, waiting for transfers between devices: 6.48 us -> 2.94 us  [on_device(): lax.ppermute(message[step], axis, [(i, i ^ step) for i in range(groups)])]
    ppermute x3 -> x6, starting transfers between devices: 3.18 us -> 5.33 us  [on_device(): lax.ppermute(message[step], axis, [(i, i ^ step) for i in range(groups)])]
    pallas_call x2 -> x4, Pallas kernels: 2.91 us -> 5.04 us  [the longest x2 2.68 us: fine_section(): pl.pallas_call(lambda *refs: fine_kernel(axis, groups, chunks, chunk, *re...]
  transfers between devices with their start and end apart: 3 -> 6, of which waited for: 2 -> 3; matrix products, arithmetic and copies ran while one was open for 1% -> 2% of each run, Pallas kernels for 0% -> 12%
where the time goes in v2:
time: 13.8 us; the launch traced here: 13.6 us
  starting transfers between devices  5.33 us (39%)
  Pallas kernels  5.04 us (37%)
  waiting for transfers between devices  2.94 us (21%)
  local copies, waits for them, and re-layouts  0.26 us (2%)
    ppermute x6, starting transfers between devices, on_device(): lax.ppermute(message[step], axis, [(i, i ^ step) for i in range(groups)])  5.33 us
    ppermute x6, waiting for transfers between devices, on_device(): lax.ppermute(message[step], axis, [(i, i ^ step) for i in range(groups)])  2.94 us
    pallas_call x2, Pallas kernels, fine_section(): pl.pallas_call(lambda *refs: fine_kernel(axis, groups, chunks, chunk, *re...  2.68 us
    pallas_call x1, Pallas kernels, coarse_section(): pl.pallas_call(lambda *refs: coarse_kernel(axis, groups, chunks, *refs),...  2.02 us
    pallas_call x1, Pallas kernels, coarse_section(): pl.pallas_call(lambda *refs: coarse_rest_kernel(axis, groups, chunks, chu...  0.33 us
  transfers between devices with their start and end apart: 6, of which 3 were waited for; matrix products, arithmetic and copies ran while one was open for 2% of the time, Pallas kernels for 12%

profile of v2, /device:TPU:0, one launch (start us, length us, event | category | flops | bytes accessed | tf_op | source)
XLA Modules:
  0.0 13.6 jit_solution(15453068233246655865)
XLA Ops:
  0.0 2.0 %coarse.1 = (f32[136,128]{1,0:T(8,128)S(1)}, f32[136,128]{1,0:T(8,128)S(1)}, f32[136,128]{1,0:T(8,128)S(1)}, f32[136,128]{1,0:T(8,128)S(1)}, bf16[2,256,256]{2,1...) custom-call(f32[1024,128]{1,0:T(8,128)} %bitcast.15, f32[16,64]{1,0:T(8,128)} %refs_1_.3, ...), custom_call_target="tpu_custom_call" | custom-call | flops 2000000 | bytes 1000000 | tf_op jit(solution)/shard_map/coarse/pallas_call | solution.py:186
  2.0 0.6 %collective-permute-start.3 = (f32[136,128]{1,0:T(8,128)S(1)}, f32[136,128]{1,0:T(8,128)S(1)}, u32[]{:S(2)}, u32[]{:S(2)}) collective-permute-start(f32[136,128]{1,0:T(8,128)S(1)} %get-tuple-element.24), channel_id=1, source_target_pairs={{0,1},{1,0},{2,3},{3,2},{4,5},{5,4},{6,7},{7,6},{8,9},{9,8},{10,11... | collective-permute-start | bytes 208904 | tf_op jit(solution)/shard_map/ppermute | solution.py:345
  2.6 2.6 %collective-permute-start.4 = (f32[136,128]{1,0:T(8,128)S(1)}, f32[136,128]{1,0:T(8,128)S(1)}, u32[]{:S(2)}, u32[]{:S(2)}) collective-permute-start(f32[136,128]{1,0:T(8,128)S(1)} %get-tuple-element.25), channel_id=1, source_target_pairs={{0,2},{1,3},{2,0},{3,1},{4,6},{5,7},{6,4},{7,5},{8,10},{9,11},{10,... | collective-permute-start | bytes 208904 | tf_op jit(solution)/shard_map/ppermute | solution.py:345
  5.2 0.0 collective-permute-start.5
  5.2 0.3 %coarse_rest.1 = (f32[136,128]{1,0:T(8,128)S(1)}, f32[136,128]{1,0:T(8,128)S(1)}, f32[136,128]{1,0:T(8,128)S(1)}, f32[136,128]{1,0:T(8,128)S(1)}) custom-call(bf16[2,256,256]{2,1,0:T(8,128)(2,1)S(1)} %get-tuple-element.16.refs_0_, bf16[528,256]{1,0:T(8,128)(2,1)S(1)} %get-tuple-element.17.refs_1_, bf16[528,256]{1,0:T(8,128)(2,1)S(1)} %get-tuple-element.18.refs_2_), custom_call_target="tpu_custom_call" | custom-call | flops 2000000 | bytes 1000000 | tf_op jit(solution)/shard_map/coarse_rest/pallas_call | solution.py:206
  5.5 0.2 %collective-permute-start = (f32[136,128]{1,0:T(8,128)S(1)}, f32[136,128]{1,0:T(8,128)S(1)}, u32[]{:S(2)}, u32[]{:S(2)}) collective-permute-start(f32[136,128]{1,0:T(8,128)S(1)} %get-tuple-element.20), channel_id=1, source_target_pairs={{0,1},{1,0},{2,3},{3,2},{4,5},{5,4},{6,7},{7,6},{8,9},{9,8},{10,11... | collective-permute-start | bytes 208904 | tf_op jit(solution)/shard_map/ppermute | solution.py:345
  5.7 1.9 %collective-permute-start.1 = (f32[136,128]{1,0:T(8,128)S(1)}, f32[136,128]{1,0:T(8,128)S(1)}, u32[]{:S(2)}, u32[]{:S(2)}) collective-permute-start(f32[136,128]{1,0:T(8,128)S(1)} %get-tuple-element.21), channel_id=1, source_target_pairs={{0,2},{1,3},{2,0},{3,1},{4,6},{5,7},{6,4},{7,5},{8,10},{9,11},{10,... | collective-permute-start | bytes 208904 | tf_op jit(solution)/shard_map/ppermute | solution.py:345
  7.7 0.0 collective-permute-done.3.refs_5_
  7.7 0.0 collective-permute-start.2
  7.7 0.0 copy-done.3
  7.7 0.1 %copy.10 = f32[12,512]{0,1:T(8,128)S(1)} copy(f32[12,512]{1,0:T(8,128)S(1)} %copy-done.3) | data formatting | bytes 49152 | tf_op args[2]
  7.8 0.0 copy-start
  7.9 0.0 copy-start.1
  7.9 0.0 copy-start.2
  7.9 0.1 copy.11
  8.0 0.0 collective-permute-done.4.refs_6_
  8.0 1.3 %collective-permute-done.5.refs_7_ = f32[136,128]{1,0:T(8,128)S(1)} collective-permute-done((f32[136,128]{1,0:T(8,128)S(1)}, f32[136,128]{1,0:T(8,128)S(1)}, u32[]{:S(2)}, u32[]{:S(2)}) %collective-permute-start.5) | collective-permute-done | bytes 69664 | tf_op jit(solution)/shard_map/ppermute | solution.py:345
  9.3 0.0 copy-done
  9.3 0.0 copy-done.1
  9.3 1.3 %fine.2.refs_8_ = f32[2,512,128]{2,1,0:T(8,128)} custom-call(f32[4,12,128]{2,1,0:T(8,128)S(1)} %bitcast.12, bf16[256,256]{1,0:T(8,128)(2,1)S(1)} %copy-done.1, bf16[256,256]{1,0:T(8,128)(2,1)S(1)} %copy-done, f32[4,2,128]{2,1,0:T(2,128)S(1)} %copy-done.2, f32[136,128]{1,0:T(8,128)S(1)} %get-tuple-element.23.refs_4_, ...), custom_call_target="tpu_custom_call" | custom-call | flops 2000000 | bytes 1000000 | tf_op jit(solution)/shard_map/fine/pallas_call | solution.py:312
  10.7 0.0 collective-permute-done.refs_5_
  10.7 0.8 %collective-permute-done.1.refs_6_ = f32[136,128]{1,0:T(8,128)S(1)} collective-permute-done((f32[136,128]{1,0:T(8,128)S(1)}, f32[136,128]{1,0:T(8,128)S(1)}, u32[]{:S(2)}, u32[]{:S(2)}) %collective-permute-start.1) | collective-permute-done | bytes 69664 | tf_op jit(solution)/shard_map/ppermute | solution.py:345
  11.5 0.8 %collective-permute-done.2.refs_7_ = f32[136,128]{1,0:T(8,128)S(1)} collective-permute-done((f32[136,128]{1,0:T(8,128)S(1)}, f32[136,128]{1,0:T(8,128)S(1)}, u32[]{:S(2)}, u32[]{:S(2)}) %collective-permute-start.2) | collective-permute-done | bytes 69664 | tf_op jit(solution)/shard_map/ppermute | solution.py:345
  12.3 1.3 %fine.3 = f32[2,512,128]{2,1,0:T(8,128)} custom-call(f32[4,12,128]{2,1,0:T(8,128)S(1)} %bitcast.13, bf16[256,256]{1,0:T(8,128)(2,1)S(1)} %copy-done.1, bf16[256,256]{1,0:T(8,128)(2,1)S(1)} %copy-done, f32[4,2,128]{2,1,0:T(2,128)S(1)} %copy-done.2, f32[136,128]{1,0:T(8,128)S(1)} %get-tuple-element.19.refs_4_, ...), custom_call_target="tpu_custom_call", output_to_operand_aliasing={{}: (8, {})} | custom-call | flops 2000000 | bytes 1000000 | tf_op jit(solution)/shard_map/fine/pallas_call | solution.py:312
  (2 shorter events, 0.0 us)
Async XLA Ops:
  2.0 5.7 %collective-permute-start.3 = (f32[136,128]{1,0:T(8,128)S(1)}, f32[136,128]{1,0:T(8,128)S(1)}, u32[]{:S(2)}, u32[]{:S(2)}) collective-permute-start(f32[136,128]{1,0:T(8,128)S(1)} %get-tuple-element.24), channel_id=1, source_target_pairs={{0,1},{1,0},{2,3},{3,2},{4,5},{5,4},{6,7},{7,6},{8,9},{9,8},{10,11... | collective-permute-start | bytes 208904 | tf_op jit(solution)/shard_map/ppermute | solution.py:345
  2.6 5.4 %collective-permute-start.4 = (f32[136,128]{1,0:T(8,128)S(1)}, f32[136,128]{1,0:T(8,128)S(1)}, u32[]{:S(2)}, u32[]{:S(2)}) collective-permute-start(f32[136,128]{1,0:T(8,128)S(1)} %get-tuple-element.25), channel_id=1, source_target_pairs={{0,2},{1,3},{2,0},{3,1},{4,6},{5,7},{6,4},{7,5},{8,10},{9,11},{10,... | collective-permute-start | bytes 208904 | tf_op jit(solution)/shard_map/ppermute | solution.py:345
  5.2 4.1 %collective-permute-start.5 = (f32[136,128]{1,0:T(8,128)S(1)}, f32[136,128]{1,0:T(8,128)S(1)}, u32[]{:S(2)}, u32[]{:S(2)}) collective-permute-start(f32[136,128]{1,0:T(8,128)S(1)} %get-tuple-element.26), channel_id=1, source_target_pairs={{0,3},{1,2},{2,1},{3,0},{4,7},{5,6},{6,5},{7,4},{8,11},{9,10},{10,... | collective-permute-start | bytes 208904 | tf_op jit(solution)/shard_map/ppermute | solution.py:345
  5.2 2.5 %copy-start.3 = (f32[12,512]{1,0:T(8,128)S(1)}, f32[12,512]{1,0:T(8,128)}, u32[]{:S(2)}) copy-start(f32[12,512]{1,0:T(8,128)} %param.9) | copy-start | bytes 73732
  5.5 5.1 %collective-permute-start = (f32[136,128]{1,0:T(8,128)S(1)}, f32[136,128]{1,0:T(8,128)S(1)}, u32[]{:S(2)}, u32[]{:S(2)}) collective-permute-start(f32[136,128]{1,0:T(8,128)S(1)} %get-tuple-element.20), channel_id=1, source_target_pairs={{0,1},{1,0},{2,3},{3,2},{4,5},{5,4},{6,7},{7,6},{8,9},{9,8},{10,11... | collective-permute-start | bytes 208904 | tf_op jit(solution)/shard_map/ppermute | solution.py:345
  5.7 5.7 %collective-permute-start.1 = (f32[136,128]{1,0:T(8,128)S(1)}, f32[136,128]{1,0:T(8,128)S(1)}, u32[]{:S(2)}, u32[]{:S(2)}) collective-permute-start(f32[136,128]{1,0:T(8,128)S(1)} %get-tuple-element.21), channel_id=1, source_target_pairs={{0,2},{1,3},{2,0},{3,1},{4,6},{5,7},{6,4},{7,5},{8,10},{9,11},{10,... | collective-permute-start | bytes 208904 | tf_op jit(solution)/shard_map/ppermute | solution.py:345
  7.7 4.6 %collective-permute-start.2 = (f32[136,128]{1,0:T(8,128)S(1)}, f32[136,128]{1,0:T(8,128)S(1)}, u32[]{:S(2)}, u32[]{:S(2)}) collective-permute-start(f32[136,128]{1,0:T(8,128)S(1)} %get-tuple-element.22), channel_id=1, source_target_pairs={{0,3},{1,2},{2,1},{3,0},{4,7},{5,6},{6,5},{7,4},{8,11},{9,10},{10,... | collective-permute-start | bytes 208904 | tf_op jit(solution)/shard_map/ppermute | solution.py:345
  7.8 1.5 %copy-start = (bf16[256,256]{1,0:T(8,128)(2,1)S(1)}, bf16[256,256]{1,0:T(8,128)(2,1)}, u32[]{:S(2)}) copy-start(bf16[256,256]{1,0:T(8,128)(2,1)} %constant.10.clone.refs_2_) | copy-start | bytes 393220
  7.9 1.5 %copy-start.1 = (bf16[256,256]{1,0:T(8,128)(2,1)S(1)}, bf16[256,256]{1,0:T(8,128)(2,1)}, u32[]{:S(2)}) copy-start(bf16[256,256]{1,0:T(8,128)(2,1)} %constant.9.clone.refs_1_) | copy-start | bytes 393220
  7.9 1.5 %copy-start.2 = (f32[4,2,128]{2,1,0:T(2,128)S(1)}, f32[4,2,128]{2,1,0:T(2,128)}, u32[]{:S(2)}) copy-start(f32[4,2,128]{2,1,0:T(2,128)} %constant.11.clone.refs_3_) | copy-start | bytes 12292

commit v3 on v1

v3 whole, which is shorter than its diff:
```python
import math

import jax
import jax.numpy as jnp
import numpy as np
from jax import lax
from jax.experimental import pallas as pl
from jax.experimental.pallas import tpu as pltpu
from jax.sharding import PartitionSpec as P

LANES = 128
F32, BF16 = jnp.float32, jnp.bfloat16


def split_table(table):
    high = np.asarray(table, np.float32).astype(jnp.bfloat16)
    low = (np.asarray(table, np.float64) - high.astype(np.float64)).astype(np.float32).astype(jnp.bfloat16)
    return high, low


def complex_table(turns, points, factor):
    angle = (turns % points) * (2.0 * math.pi / points)
    return np.cos(angle) * factor, -np.sin(angle) * factor


def coarse_table(channels, groups):
    halves, per = LANES // channels, channels // groups
    k, p = np.arange(channels), np.arange(channels)
    real, imag = complex_table(k[:, None] * p[None, :], channels, 1.0 / math.sqrt(channels))
    table = np.zeros((groups, 2, halves, per, 2, halves, channels))
    real, imag = real.reshape(-1, per, channels), imag.reshape(-1, per, channels)
    for half in range(halves):
        table[:, 0, half, :, 0, half] = real
        table[:, 0, half, :, 1, half] = -imag
        table[:, 1, half, :, 0, half] = imag
        table[:, 1, half, :, 1, half] = real
    return table.reshape(2 * LANES, 2 * LANES)


def fine_tables(fine):
    radix = fine // LANES
    i = np.arange(LANES)
    real, imag = complex_table(i[:, None] * i[None, :], LANES, 1.0 / math.sqrt(fine))
    table = np.block([[real, imag], [-imag, real]])
    real, imag = complex_table(np.arange(radix)[:, None] * i[None, :], fine, 1.0)
    return table, np.stack([real, imag], axis=1).astype(np.float32)


def split_value(value):
    high = value.astype(BF16)
    return high, (value - high.astype(F32)).astype(BF16)


def dot_nt(left, right):
    return lax.dot_general(left, right, (((1,), (1,)), ((), ())), preferred_element_type=F32)


def dot_nn(left, right):
    return lax.dot_general(left, right, (((1,), (0,)), ((), ())), preferred_element_type=F32)


VMEM = pl.BlockSpec(memory_space=pltpu.VMEM)
ANY = pl.BlockSpec(memory_space=pl.ANY)
PARAMS = pltpu.CompilerParams(vmem_limit_bytes=24 * 1024 * 1024)


def in_vmem(value):
    return pltpu.with_memory_space_constraint(value, pltpu.VMEM)


PAD = 16
PIECES = 4
COST = pl.CostEstimate(flops=2000000, bytes_accessed=1000000, transcendentals=0)


def in_hbm(value):
    return pltpu.with_memory_space_constraint(value, pltpu.HBM)


def pick_rows(table_ref, half, axis, groups):
    me = lax.axis_index(axis)
    span = 2 * LANES // groups
    picks = [pl.multiple_of((me ^ step) * span, span) for step in range(groups)]
    return jnp.concatenate([table_ref[half, pl.ds(pick, span), :] for pick in picks], axis=0)


def filter_rows(xs, ys, bs, taps, base, block, origin):
    channels = LANES // 2
    lower = lax.broadcasted_iota(jnp.int32, (1, LANES), 1) < channels
    now = xs[PAD + base : PAD + base + block]
    before = xs[PAD + base - 2 : PAD + base + block - 2]
    at = base - origin
    ys[PAD + at : PAD + at + block] = pltpu.roll(jnp.where(lower, now, before), channels, 1)
    if bs is None:
        return
    summed = None
    for parity, source, start in ((0, xs, PAD + base), (1, ys, PAD + at)):
        for shift in range(taps.shape[0] // 4):
            low = start - 2 * shift - 8
            piece = source[low : low + block + 8]
            near = taps[2 * shift + parity][None, :]
            far = taps[2 * (shift + 4) + parity][None, :]
            term = piece[8:] * near + piece[:block] * far
            summed = term if summed is None else summed + term
    bs[at : at + block] = summed


def gather_rows(bs, base, count):
    parts = [
        jnp.concatenate([bs[pl.ds(base + 2 * a + part, count, stride=4), :] for part in range(2)], axis=1)
        for a in range(2)
    ]
    return jnp.concatenate(parts, axis=0)


def send_frame(groups, high, low, gathered, outs):
    span = 2 * LANES // groups
    bh, bl = split_value(gathered)
    result = dot_nt(high, bh) + dot_nt(low, bh) + dot_nt(high, bl)
    for step in range(groups):
        for a in range(2):
            outs[step][a * span : (a + 1) * span] = result[step * span : (step + 1) * span, a * LANES : (a + 1) * LANES]


def coarse_kernel(axis, groups, x_hbm, taps_hbm, table_hbm, *rest):
    outs, (table_ref, taps_out, xs, taps_ref, ys, bs, yt, bt, sems) = rest[:groups], rest[groups:]
    rows = x_hbm.shape[0]
    span = 2 * LANES // groups
    step = rows // PIECES
    loads = [
        pltpu.make_async_copy(x_hbm.at[pl.ds(i * step, step)], xs.at[pl.ds(PAD + i * step, step)], sems.at[i])
        for i in range(PIECES)
    ]
    get_taps = pltpu.make_async_copy(taps_hbm, taps_ref, sems.at[PIECES])
    get_table = pltpu.make_async_copy(table_hbm, table_ref, sems.at[PIECES + 1])
    get_taps.start()
    for load in loads[: PIECES // 2]:
        load.start()
    get_table.start()
    for load in loads[PIECES // 2 :]:
        load.start()
    zeros = jnp.zeros((PAD, LANES), F32)
    xs[:PAD] = zeros
    xs[PAD + rows :] = zeros
    ys[:PAD] = zeros
    get_taps.wait()
    taps = taps_ref[...]
    taps = jnp.concatenate([taps, taps], axis=1)
    taps_out[...] = taps
    block = 64
    for i in range(PIECES // 2):
        loads[i].wait()
        for base in range(i * step, (i + 1) * step, block):
            filter_rows(xs, ys, bs, taps, base, block, 0)
    for load in loads[PIECES // 2 :]:
        load.wait()
    get_table.wait()
    high, low = pick_rows(table_ref, 0, axis, groups), pick_rows(table_ref, 1, axis, groups)
    send_frame(groups, high, low, gather_rows(bs, 0, LANES), outs)
    yt[:PAD] = zeros
    filter_rows(xs, yt, None, taps, rows - 16, 16, rows - 16)
    filter_rows(xs, yt, bt, taps, rows, 16, rows - 16)
    th, tl = split_value(gather_rows(bt, 16, 4))
    tail = dot_nt(th, high) + dot_nt(th, low) + dot_nt(tl, high)
    for step in range(groups):
        at = step * span // LANES * LANES
        outs[step][2 * span : 2 * span + 8] = tail[:, at : at + LANES]


def coarse_rest_kernel(axis, groups, table_ref, taps_ref, xs, *rest):
    outs, (ys, bs) = rest[:groups], rest[groups:]
    rows = xs.shape[0] - 2 * PAD
    taps = taps_ref[...]
    block = 64
    origin = rows // 2 - 16
    filter_rows(xs, ys, None, taps, origin, 16, origin)
    for base in range(rows // 2, rows, block):
        filter_rows(xs, ys, bs, taps, base, block, origin)
    high, low = pick_rows(table_ref, 0, axis, groups), pick_rows(table_ref, 1, axis, groups)
    send_frame(groups, high, low, gather_rows(bs, 16, LANES), outs)


def coarse_section(signal, coarse_taps, axis, groups):
    length = signal.shape[1]
    taps_count, channels = coarse_taps.shape
    count = length // LANES
    rows = signal.reshape(2, count, LANES).transpose(1, 0, 2).reshape(2 * count, LANES)
    table = jnp.asarray(np.stack(split_table(coarse_table(channels, groups))))
    span = 2 * LANES // groups
    first = pl.pallas_call(
        lambda *refs: coarse_kernel(axis, groups, *refs),
        out_shape=[pltpu.VMEM((2 * span + 8, LANES), F32)] * groups
        + [
            pltpu.VMEM((2, 2 * LANES, 2 * LANES), BF16),
            pltpu.VMEM((taps_count, LANES), F32),
            pltpu.VMEM((2 * count + 2 * PAD, LANES), F32),
        ],
        in_specs=[ANY] * 3,
        out_specs=[VMEM] * (groups + 3),
        scratch_shapes=[
            pltpu.VMEM((taps_count, channels), F32),
            pltpu.VMEM((count + PAD, LANES), F32),
            pltpu.VMEM((count, LANES), F32),
            pltpu.VMEM((PAD + 32, LANES), F32),
            pltpu.VMEM((32, LANES), F32),
            pltpu.SemaphoreType.DMA((PIECES + 2,)),
        ],
        compiler_params=PARAMS,
        cost_estimate=COST,
        name="coarse",
    )(in_hbm(rows), in_hbm(coarse_taps), in_hbm(table))
    second = pl.pallas_call(
        lambda *refs: coarse_rest_kernel(axis, groups, *refs),
        out_shape=[pltpu.VMEM((2 * span, LANES), F32)] * groups,
        in_specs=[VMEM] * 3,
        out_specs=[VMEM] * groups,
        scratch_shapes=[
            pltpu.VMEM((count + 16 + PAD, LANES), F32),
            pltpu.VMEM((count + 16, LANES), F32),
        ],
        compiler_params=PARAMS,
        cost_estimate=COST,
        name="coarse_rest",
    )(*[in_vmem(value) for value in first[groups:]])
    return first[:groups], second


def place(axis, groups, pieces, xs):
    span = 2 * LANES // groups
    me = lax.axis_index(axis)
    for step in range(groups):
        for a in range(2):
            xs[me ^ step, a] = pieces[step][a * span : (a + 1) * span]


def terms(xs, taps, parity, m, a, rows):
    taps_count = len(taps)
    return [xs[g, a, rows] * taps[m - 2 * g - parity] for g in range((m - parity) // 2, -1, -1) if m - 2 * g - parity < taps_count] if m >= parity else []


def fine_start_kernel(axis, groups, taps_ref, *refs):
    pieces, (out_ref, xs) = refs[:groups], refs[groups:]
    span = 2 * LANES // groups
    per, frames = span // 4, 2 * groups
    me = lax.axis_index(axis)
    place(axis, groups, pieces, xs)
    for step in range(groups):
        tail = jnp.transpose(pieces[step][2 * span : 2 * span + 8])
        at = step * span % LANES
        tail = tail[at : at + span]
        owner = (me ^ step) + 1
        for a in range(2):
            xs[owner, a, :, 0:4] = xs[owner, a, :, 0:4] + tail[:, 4 * a : 4 * a + 4]
    taps_count = taps_ref.shape[1]
    for a in range(2):
        for h in range(2):
            phase = 2 * a + h
            taps = [taps_ref[phase, j : j + 1] for j in range(taps_count)]
            for part in range(2):
                rows = slice((2 * part + h) * per, (2 * part + h + 1) * per)
                for m in range(frames):
                    out_ref[phase, part, m * per : (m + 1) * per] = sum(terms(xs, taps, 0, m, a, rows))


def fine_kernel(axis, groups, taps_ref, high_ref, low_ref, turn_ref, acc_ref, *refs):
    pieces, (out_hbm, xs, fs, yh, yl, zs, os, sem) = refs[:groups], refs[groups:]
    span = 2 * LANES // groups
    per, frames = span // 4, 2 * groups
    taps_count = taps_ref.shape[1]
    place(axis, groups, pieces, xs)
    for a in range(2):
        for h in range(2):
            phase = 2 * a + h
            taps = [taps_ref[phase, j : j + 1] for j in range(taps_count)]
            for part in range(2):
                rows = slice((2 * part + h) * per, (2 * part + h + 1) * per)
                for m in range(frames):
                    at = m * per
                    fs[phase, part, at : at + per] = sum(terms(xs, taps, 1, m, a, rows), acc_ref[phase, part, at : at + per])
    high, low = high_ref[...], low_ref[...]
    blocks = frames // 8
    share = per // SHARES
    height = share * frames
    copies = []
    for turn in range(SHARES):
        for phase in range(4):
            columns = []
            for part in range(2):
                picked = [fs[phase, part, pl.ds(turn * share + k, frames, stride=per), :] for k in range(share)]
                columns.append(jnp.concatenate(picked, axis=0))
            first, second = split_value(jnp.concatenate(columns, axis=1))
            yh[turn, phase * height : (phase + 1) * height] = first
            yl[turn, phase * height : (phase + 1) * height] = second
        zs[turn] = dot_nn(yh[turn], high) + dot_nn(yl[turn], high) + dot_nn(yh[turn], low)
        for at in range(0, height, 8):
            z = []
            for phase in range(4):
                row = phase * height + at
                real, imag = zs[turn, row : row + 8, :LANES], zs[turn, row : row + 8, LANES:]
                if phase:
                    c, s = turn_ref[phase, 0:1], turn_ref[phase, 1:2]
                    real, imag = real * c - imag * s, real * s + imag * c
                z.append((real, imag))
            (ar, ai), (br, bi), (cr, ci), (dr, di) = z
            pr, pi, qr, qi = ar + cr, ai + ci, ar - cr, ai - ci
            ur, ui, vr, vi = br + dr, bi + di, br - dr, bi - di
            reals = (pr + ur, qr + vi, pr - ur, qr - vi)
            imags = (pi + ui, qi - vr, pi - ui, qi + vr)
            for part, values in enumerate((reals, imags)):
                for r, value in enumerate(values):
                    row = ((turn * share * blocks + at // 8) * 4 + r) * 8
                    os[part, row : row + 8, :] = value
        length = share * blocks * 32
        for part in range(2):
            place_of = pl.ds(turn * length, length)
            copy = pltpu.make_async_copy(os.at[part, place_of], out_hbm.at[part, place_of], sem.at[2 * turn + part])
            copy.start()
            copies.append(copy)
    for copy in copies:
        copy.wait()


SHARES = 2


def fine_section(moved, fine_taps, axis, groups):
    taps_count, fine = fine_taps.shape
    span = 2 * LANES // groups
    per, frames = span // 4, 2 * groups
    taps = in_vmem(fine_taps.reshape(taps_count, LANES, fine // LANES).transpose(2, 0, 1))
    table, turns = fine_tables(fine)
    high, low = split_table(table)
    started = pl.pallas_call(
        lambda *refs: fine_start_kernel(axis, groups, *refs),
        out_shape=pltpu.VMEM((4, 2, frames * per, LANES), F32),
        in_specs=[VMEM] * (1 + groups),
        out_specs=VMEM,
        scratch_shapes=[pltpu.VMEM((groups + 1, 2, span, LANES), F32)],
        compiler_params=PARAMS,
        cost_estimate=COST,
        name="fine_start",
    )(taps, *[in_vmem(value) for value in moved[0]])
    height = 4 * frames * per // SHARES
    length = per * frames * 4
    shared = [jnp.asarray(high), jnp.asarray(low), jnp.asarray(turns), started]
    out = pl.pallas_call(
        lambda *refs: fine_kernel(axis, groups, *refs),
        out_shape=pltpu.HBM((2, length, LANES), F32),
        in_specs=[VMEM] * (5 + groups),
        out_specs=ANY,
        scratch_shapes=[
            pltpu.VMEM((groups + 1, 2, span, LANES), F32),
            pltpu.VMEM((4, 2, frames * per, LANES), F32),
            pltpu.VMEM((SHARES, height, 2 * LANES), BF16),
            pltpu.VMEM((SHARES, height, 2 * LANES), BF16),
            pltpu.VMEM((SHARES, height, 2 * LANES), F32),
            pltpu.VMEM((2, length, LANES), F32),
            pltpu.SemaphoreType.DMA((2 * SHARES,)),
        ],
        compiler_params=PARAMS,
        cost_estimate=COST,
        name="fine",
    )(taps, *[in_vmem(value) for value in shared + list(moved[1])])
    out = out.reshape(2, per, frames // 8, 4, 8, LANES).transpose(0, 1, 2, 4, 3, 5)
    return out.reshape(2, per, frames, 4 * LANES)


def solution(mesh):
    axis = "tm"
    groups = mesh.shape[axis]

    def on_device(signal, coarse_taps, fine_taps):
        moved = []
        for message in coarse_section(signal, coarse_taps, axis, groups):
            arrived = [message[0]]
            for step in range(1, groups):
                arrived.append(lax.ppermute(message[step], axis, [(i, i ^ step) for i in range(groups)]))
            moved.append(arrived)
        return fine_section(moved, fine_taps, axis, groups)

    return jax.shard_map(
        on_device,
        mesh=mesh,
        in_specs=(P(None, ("streams", "tm")), P(), P()),
        out_specs=P(None, "tm", "streams", None),
        check_vma=False,
    )
```

time: 16.7 us -> 13.7 us (0.82)
  local copies, waits for them, and re-layouts: 3.81 us -> 0.26 us
  waiting for transfers between devices: 6.48 us -> 3.75 us
  starting transfers between devices: 3.18 us -> 5.35 us
  Pallas kernels: 2.91 us -> 4.05 us
    unnamed x17 -> x9, local copies, waits for them, and re-layouts: 3.71 us -> 0.15 us
    ppermute x3 -> x6, waiting for transfers between devices: 6.48 us -> 3.75 us  [on_device(): lax.ppermute(message[step], axis, [(i, i ^ step) for i in range(groups)])]
    ppermute x3 -> x6, starting transfers between devices: 3.18 us -> 5.35 us  [on_device(): lax.ppermute(message[step], axis, [(i, i ^ step) for i in range(groups)])]
    pallas_call x2 -> x4, Pallas kernels: 2.91 us -> 4.05 us  [the longest x1 1.67 us: coarse_section(): pl.pallas_call(lambda *refs: coarse_kernel(axis, groups, *refs), out_shap...]
  transfers between devices with their start and end apart: 3 -> 6, of which waited for: 2 -> 3; matrix products, arithmetic and copies ran while one was open for 1% -> 2% of each run, Pallas kernels for 0% -> 7%
where the time goes in v3:
time: 13.7 us; the launch traced here: 13.5 us
  starting transfers between devices  5.35 us (39%)
  Pallas kernels  4.05 us (30%)
  waiting for transfers between devices  3.75 us (27%)
  local copies, waits for them, and re-layouts  0.26 us (2%)
    ppermute x6, starting transfers between devices, on_device(): lax.ppermute(message[step], axis, [(i, i ^ step) for i in range(groups)])  5.35 us
    ppermute x6, waiting for transfers between devices, on_device(): lax.ppermute(message[step], axis, [(i, i ^ step) for i in range(groups)])  3.75 us
    pallas_call x1, Pallas kernels, coarse_section(): pl.pallas_call(lambda *refs: coarse_kernel(axis, groups, *refs), out_shap...  1.67 us
    pallas_call x1, Pallas kernels, fine_section(): pl.pallas_call(lambda *refs: fine_kernel(axis, groups, *refs), out_shape=...  1.42 us
    pallas_call x1, Pallas kernels, coarse_section(): pl.pallas_call(lambda *refs: coarse_rest_kernel(axis, groups, *refs), out...  0.61 us
    pallas_call x1, Pallas kernels, fine_section(): pl.pallas_call(lambda *refs: fine_start_kernel(axis, groups, *refs), out_...  0.36 us
  transfers between devices with their start and end apart: 6, of which 3 were waited for; matrix products, arithmetic and copies ran while one was open for 2% of the time, Pallas kernels for 7%

profile of v3, /device:TPU:0, one launch (start us, length us, event | category | flops | bytes accessed | tf_op | source)
XLA Modules:
  0.0 13.5 jit_solution(8014243709093552404)
XLA Ops:
  0.0 1.7 %coarse.1 = (f32[136,128]{1,0:T(8,128)S(1)}, f32[136,128]{1,0:T(8,128)S(1)}, f32[136,128]{1,0:T(8,128)S(1)}, f32[136,128]{1,0:T(8,128)S(1)}, bf16[2,256,256]{2,1...) custom-call(f32[1024,128]{1,0:T(8,128)} %bitcast.15, f32[16,64]{1,0:T(8,128)} %refs_1_.2, ...), custom_call_target="tpu_custom_call" | custom-call | flops 2000000 | bytes 1000000 | tf_op jit(solution)/shard_map/coarse/pallas_call | solution.py:190
  1.7 0.6 %collective-permute-start = (f32[136,128]{1,0:T(8,128)S(1)}, f32[136,128]{1,0:T(8,128)S(1)}, u32[]{:S(2)}, u32[]{:S(2)}) collective-permute-start(f32[136,128]{1,0:T(8,128)S(1)} %get-tuple-element.17), channel_id=1, source_target_pairs={{0,1},{1,0},{2,3},{3,2},{4,5},{5,4},{6,7},{7,6},{8,9},{9,8},{10,11... | collective-permute-start | bytes 208904 | tf_op jit(solution)/shard_map/ppermute | solution.py:377
  2.2 2.6 %collective-permute-start.1 = (f32[136,128]{1,0:T(8,128)S(1)}, f32[136,128]{1,0:T(8,128)S(1)}, u32[]{:S(2)}, u32[]{:S(2)}) collective-permute-start(f32[136,128]{1,0:T(8,128)S(1)} %get-tuple-element.18), channel_id=1, source_target_pairs={{0,2},{1,3},{2,0},{3,1},{4,6},{5,7},{6,4},{7,5},{8,10},{9,11},{10,... | collective-permute-start | bytes 208904 | tf_op jit(solution)/shard_map/ppermute | solution.py:377
  4.8 0.0 collective-permute-start.2
  4.9 0.0 copy-start.3
  4.9 0.6 %coarse_rest.1 = (f32[128,128]{1,0:T(8,128)S(1)}, f32[128,128]{1,0:T(8,128)S(1)}, f32[128,128]{1,0:T(8,128)S(1)}, f32[128,128]{1,0:T(8,128)S(1)}) custom-call(bf16[2,256,256]{2,1,0:T(8,128)(2,1)S(1)} %get-tuple-element.20.refs_0_, f32[16,128]{1,0:T(8,128)S(1)} %get-tuple-element.21.refs_1_, f32[1056,128]{1,0:T(8,128)S(1)} %get-tuple-element.22.refs_2_), custom_call_target="tpu_custom_call" | custom-call | flops 2000000 | bytes 1000000 | tf_op jit(solution)/shard_map/coarse_rest/pallas_call | solution.py:212
  5.5 0.2 %collective-permute-start.3 = (f32[128,128]{1,0:T(8,128)S(1)}, f32[128,128]{1,0:T(8,128)S(1)}, u32[]{:S(2)}, u32[]{:S(2)}) collective-permute-start(f32[128,128]{1,0:T(8,128)S(1)} %get-tuple-element.24), channel_id=1, source_target_pairs={{0,1},{1,0},{2,3},{3,2},{4,5},{5,4},{6,7},{7,6},{8,9},{9,8},{10,11... | collective-permute-start | bytes 196616 | tf_op jit(solution)/shard_map/ppermute | solution.py:377
  5.7 1.9 %collective-permute-start.4 = (f32[128,128]{1,0:T(8,128)S(1)}, f32[128,128]{1,0:T(8,128)S(1)}, u32[]{:S(2)}, u32[]{:S(2)}) collective-permute-start(f32[128,128]{1,0:T(8,128)S(1)} %get-tuple-element.25), channel_id=1, source_target_pairs={{0,2},{1,3},{2,0},{3,1},{4,6},{5,7},{6,4},{7,5},{8,10},{9,11},{10,... | collective-permute-start | bytes 196616 | tf_op jit(solution)/shard_map/ppermute | solution.py:377
  7.6 0.0 collective-permute-done.refs_2_
  7.6 0.0 collective-permute-start.5
  7.7 0.0 copy-done.3
  7.7 0.1 %copy.9 = f32[12,512]{0,1:T(8,128)S(1)} copy(f32[12,512]{1,0:T(8,128)S(1)} %copy-done.3) | data formatting | bytes 49152 | tf_op args[2]
  7.8 0.1 copy.10
  7.9 0.0 collective-permute-done.1.refs_3_
  7.9 1.0 %collective-permute-done.2.refs_4_ = f32[136,128]{1,0:T(8,128)S(1)} collective-permute-done((f32[136,128]{1,0:T(8,128)S(1)}, f32[136,128]{1,0:T(8,128)S(1)}, u32[]{:S(2)}, u32[]{:S(2)}) %collective-permute-start.2) | collective-permute-done | bytes 69664 | tf_op jit(solution)/shard_map/ppermute | solution.py:377
  9.0 0.0 copy-start
  9.0 0.4 %fine_start.1.refs_4_ = f32[4,2,128,128]{3,2,1,0:T(8,128)S(1)} custom-call(f32[4,12,128]{2,1,0:T(8,128)S(1)} %bitcast.12, f32[136,128]{1,0:T(8,128)S(1)} %get-tuple-element.16.refs_1_, f32[136,128]{1,0:T(8,128)S(1)} %collective-permute-done.refs_2_, f32[136,128]{1,0:T(8,128)S(1)} %collective-permute-done.1.refs_3_, f32[136,128]{1,0:T(8,128)S(1)} %collective-permute-done.2.refs_4_), custom_call_target="tpu_custom_call" | custom-call | flops 2000000 | bytes 1000000 | tf_op jit(solution)/shard_map/fine_start/pallas_call | solution.py:333
  9.3 0.0 collective-permute-done.3.refs_6_
  9.3 1.4 %collective-permute-done.4.refs_7_ = f32[128,128]{1,0:T(8,128)S(1)} collective-permute-done((f32[128,128]{1,0:T(8,128)S(1)}, f32[128,128]{1,0:T(8,128)S(1)}, u32[]{:S(2)}, u32[]{:S(2)}) %collective-permute-start.4) | collective-permute-done | bytes 65568 | tf_op jit(solution)/shard_map/ppermute | solution.py:377
  10.8 1.3 %collective-permute-done.5.refs_8_ = f32[128,128]{1,0:T(8,128)S(1)} collective-permute-done((f32[128,128]{1,0:T(8,128)S(1)}, f32[128,128]{1,0:T(8,128)S(1)}, u32[]{:S(2)}, u32[]{:S(2)}) %collective-permute-start.5) | collective-permute-done | bytes 65568 | tf_op jit(solution)/shard_map/ppermute | solution.py:377
  12.0 0.0 copy-done
  12.0 0.0 copy-done.1
  12.0 0.0 copy-done.2
  12.1 1.4 %fine.1 = f32[2,512,128]{2,1,0:T(8,128)} custom-call(f32[4,12,128]{2,1,0:T(8,128)S(1)} %bitcast.13, bf16[256,256]{1,0:T(8,128)(2,1)S(1)} %copy-done.1, bf16[256,256]{1,0:T(8,128)(2,1)S(1)} %copy-done, f32[4,2,128]{2,1,0:T(2,128)S(1)} %copy-done.2, f32[4,2,128,128]{3,2,1,0:T(8,128)S(1)} %fine_start.1.refs_4_, f32[128,128]{1,0:T(8,128)S(1)} %get-tuple-element.23.refs_5_, ...), custom_call_target="tpu_custom_call" | custom-call | flops 2000000 | bytes 1000000 | tf_op jit(solution)/shard_map/fine/pallas_call | solution.py:346
  (2 shorter events, 0.0 us)
Async XLA Ops:
  1.7 6.0 %collective-permute-start = (f32[136,128]{1,0:T(8,128)S(1)}, f32[136,128]{1,0:T(8,128)S(1)}, u32[]{:S(2)}, u32[]{:S(2)}) collective-permute-start(f32[136,128]{1,0:T(8,128)S(1)} %get-tuple-element.17), channel_id=1, source_target_pairs={{0,1},{1,0},{2,3},{3,2},{4,5},{5,4},{6,7},{7,6},{8,9},{9,8},{10,11... | collective-permute-start | bytes 208904 | tf_op jit(solution)/shard_map/ppermute | solution.py:377
  2.2 5.7 %collective-permute-start.1 = (f32[136,128]{1,0:T(8,128)S(1)}, f32[136,128]{1,0:T(8,128)S(1)}, u32[]{:S(2)}, u32[]{:S(2)}) collective-permute-start(f32[136,128]{1,0:T(8,128)S(1)} %get-tuple-element.18), channel_id=1, source_target_pairs={{0,2},{1,3},{2,0},{3,1},{4,6},{5,7},{6,4},{7,5},{8,10},{9,11},{10,... | collective-permute-start | bytes 208904 | tf_op jit(solution)/shard_map/ppermute | solution.py:377
  4.8 4.1 %collective-permute-start.2 = (f32[136,128]{1,0:T(8,128)S(1)}, f32[136,128]{1,0:T(8,128)S(1)}, u32[]{:S(2)}, u32[]{:S(2)}) collective-permute-start(f32[136,128]{1,0:T(8,128)S(1)} %get-tuple-element.19), channel_id=1, source_target_pairs={{0,3},{1,2},{2,1},{3,0},{4,7},{5,6},{6,5},{7,4},{8,11},{9,10},{10,... | collective-permute-start | bytes 208904 | tf_op jit(solution)/shard_map/ppermute | solution.py:377
  4.9 2.8 %copy-start.3 = (f32[12,512]{1,0:T(8,128)S(1)}, f32[12,512]{1,0:T(8,128)}, u32[]{:S(2)}) copy-start(f32[12,512]{1,0:T(8,128)} %param.9) | copy-start | bytes 73732
  5.5 3.9 %collective-permute-start.3 = (f32[128,128]{1,0:T(8,128)S(1)}, f32[128,128]{1,0:T(8,128)S(1)}, u32[]{:S(2)}, u32[]{:S(2)}) collective-permute-start(f32[128,128]{1,0:T(8,128)S(1)} %get-tuple-element.24), channel_id=1, source_target_pairs={{0,1},{1,0},{2,3},{3,2},{4,5},{5,4},{6,7},{7,6},{8,9},{9,8},{10,11... | collective-permute-start | bytes 196616 | tf_op jit(solution)/shard_map/ppermute | solution.py:377
  5.7 5.1 %collective-permute-start.4 = (f32[128,128]{1,0:T(8,128)S(1)}, f32[128,128]{1,0:T(8,128)S(1)}, u32[]{:S(2)}, u32[]{:S(2)}) collective-permute-start(f32[128,128]{1,0:T(8,128)S(1)} %get-tuple-element.25), channel_id=1, source_target_pairs={{0,2},{1,3},{2,0},{3,1},{4,6},{5,7},{6,4},{7,5},{8,10},{9,11},{10,... | collective-permute-start | bytes 196616 | tf_op jit(solution)/shard_map/ppermute | solution.py:377
  7.6 4.4 %collective-permute-start.5 = (f32[128,128]{1,0:T(8,128)S(1)}, f32[128,128]{1,0:T(8,128)S(1)}, u32[]{:S(2)}, u32[]{:S(2)}) collective-permute-start(f32[128,128]{1,0:T(8,128)S(1)} %get-tuple-element.26), channel_id=1, source_target_pairs={{0,3},{1,2},{2,1},{3,0},{4,7},{5,6},{6,5},{7,4},{8,11},{9,10},{10,... | collective-permute-start | bytes 196616 | tf_op jit(solution)/shard_map/ppermute | solution.py:377
  9.0 3.1 %copy-start = (bf16[256,256]{1,0:T(8,128)(2,1)S(1)}, bf16[256,256]{1,0:T(8,128)(2,1)}, u32[]{:S(2)}) copy-start(bf16[256,256]{1,0:T(8,128)(2,1)} %constant.10.clone.refs_2_) | copy-start | bytes 393220
  9.0 3.1 %copy-start.1 = (bf16[256,256]{1,0:T(8,128)(2,1)S(1)}, bf16[256,256]{1,0:T(8,128)(2,1)}, u32[]{:S(2)}) copy-start(bf16[256,256]{1,0:T(8,128)(2,1)} %constant.9.clone.refs_1_) | copy-start | bytes 393220
  9.0 3.1 %copy-start.2 = (f32[4,2,128]{2,1,0:T(2,128)S(1)}, f32[4,2,128]{2,1,0:T(2,128)}, u32[]{:S(2)}) copy-start(f32[4,2,128]{2,1,0:T(2,128)} %constant.11.clone.refs_3_) | copy-start | bytes 12292

commit v4 on v3

v4 whole, which is shorter than its diff:
```python
import math

import jax
import jax.numpy as jnp
import numpy as np
from jax import lax
from jax.experimental import pallas as pl
from jax.experimental.pallas import tpu as pltpu
from jax.sharding import PartitionSpec as P

LANES = 128
F32, BF16 = jnp.float32, jnp.bfloat16


def split_table(table):
    high = np.asarray(table, np.float32).astype(jnp.bfloat16)
    low = (np.asarray(table, np.float64) - high.astype(np.float64)).astype(np.float32).astype(jnp.bfloat16)
    return high, low


def complex_table(turns, points, factor):
    angle = (turns % points) * (2.0 * math.pi / points)
    return np.cos(angle) * factor, -np.sin(angle) * factor


def coarse_table(channels, groups, shares):
    halves, per = LANES // channels, channels // (groups * shares)
    k, p = np.arange(channels), np.arange(channels)
    real, imag = complex_table(k[:, None] * p[None, :], channels, 1.0 / math.sqrt(channels))
    table = np.zeros((groups * shares, 2, halves, per, 2, halves, channels))
    real, imag = real.reshape(-1, per, channels), imag.reshape(-1, per, channels)
    for half in range(halves):
        table[:, 0, half, :, 0, half] = real
        table[:, 0, half, :, 1, half] = -imag
        table[:, 1, half, :, 0, half] = imag
        table[:, 1, half, :, 1, half] = real
    return table.reshape(2 * LANES, 2 * LANES)


def fine_tables(fine):
    radix = fine // LANES
    i = np.arange(LANES)
    real, imag = complex_table(i[:, None] * i[None, :], LANES, 1.0 / math.sqrt(fine))
    table = np.block([[real, imag], [-imag, real]])
    real, imag = complex_table(np.arange(radix)[:, None] * i[None, :], fine, 1.0)
    return table, np.stack([real, imag], axis=1).astype(np.float32)


def split_value(value):
    high = value.astype(BF16)
    return high, (value - high.astype(F32)).astype(BF16)


def dot_nt(left, right):
    return lax.dot_general(left, right, (((1,), (1,)), ((), ())), preferred_element_type=F32)


def dot_nn(left, right):
    return lax.dot_general(left, right, (((1,), (0,)), ((), ())), preferred_element_type=F32)


VMEM = pl.BlockSpec(memory_space=pltpu.VMEM)
ANY = pl.BlockSpec(memory_space=pl.ANY)
PARAMS = pltpu.CompilerParams(vmem_limit_bytes=24 * 1024 * 1024)


def in_vmem(value):
    return pltpu.with_memory_space_constraint(value, pltpu.VMEM)


PAD = 16
PIECES = 4
COST = pl.CostEstimate(flops=2000000, bytes_accessed=1000000, transcendentals=0)


def in_hbm(value):
    return pltpu.with_memory_space_constraint(value, pltpu.HBM)


def pick_rows(table_ref, half, axis, groups):
    me = lax.axis_index(axis)
    span = 2 * LANES // groups
    picks = [pl.multiple_of((me ^ step) * span, span) for step in range(groups)]
    return jnp.concatenate([table_ref[half, pl.ds(pick, span), :] for pick in picks], axis=0)


def filter_rows(xs, ys, bs, taps, base, block, origin):
    channels = LANES // 2
    lower = lax.broadcasted_iota(jnp.int32, (1, LANES), 1) < channels
    now = xs[PAD + base : PAD + base + block]
    before = xs[PAD + base - 2 : PAD + base + block - 2]
    at = base - origin
    ys[PAD + at : PAD + at + block] = pltpu.roll(jnp.where(lower, now, before), channels, 1)
    if bs is None:
        return
    summed = None
    for parity, source, start in ((0, xs, PAD + base), (1, ys, PAD + at)):
        for shift in range(taps.shape[0] // 4):
            low = start - 2 * shift - 8
            piece = source[low : low + block + 8]
            near = taps[2 * shift + parity][None, :]
            far = taps[2 * (shift + 4) + parity][None, :]
            term = piece[8:] * near + piece[:block] * far
            summed = term if summed is None else summed + term
    bs[at : at + block] = summed


def gather_rows(bs, base, count):
    parts = [
        jnp.concatenate([bs[pl.ds(base + 2 * a + part, count, stride=4), :] for part in range(2)], axis=1)
        for a in range(2)
    ]
    return jnp.concatenate(parts, axis=0)


def frame_blocks(groups, high, low, gathered):
    span = 2 * LANES // groups
    bh, bl = split_value(gathered)
    result = dot_nt(high, bh) + dot_nt(low, bh) + dot_nt(high, bl)
    return [
        [result[step * span : (step + 1) * span, a * LANES : (a + 1) * LANES] for a in range(2)]
        for step in range(groups)
    ]


def coarse_kernel(axis, groups, x_hbm, taps_hbm, table_hbm, *rest):
    lots = 1 + groups // 2
    outs, (table_ref, taps_out, xs, taps_ref, ys, bs, yt, bt, sems) = rest[:lots], rest[lots:]
    rows = x_hbm.shape[0]
    span = 2 * LANES // groups
    step = rows // PIECES
    loads = [
        pltpu.make_async_copy(x_hbm.at[pl.ds(i * step, step)], xs.at[pl.ds(PAD + i * step, step)], sems.at[i])
        for i in range(PIECES)
    ]
    get_taps = pltpu.make_async_copy(taps_hbm, taps_ref, sems.at[PIECES])
    get_table = pltpu.make_async_copy(table_hbm, table_ref, sems.at[PIECES + 1])
    get_taps.start()
    for load in loads[: PIECES // 2]:
        load.start()
    get_table.start()
    for load in loads[PIECES // 2 :]:
        load.start()
    zeros = jnp.zeros((PAD, LANES), F32)
    xs[:PAD] = zeros
    xs[PAD + rows :] = zeros
    ys[:PAD] = zeros
    get_taps.wait()
    taps = taps_ref[...]
    taps = jnp.concatenate([taps, taps], axis=1)
    taps_out[...] = taps
    block = 64
    for i in range(PIECES // 2):
        loads[i].wait()
        for base in range(i * step, (i + 1) * step, block):
            filter_rows(xs, ys, bs, taps, base, block, 0)
    for load in loads[PIECES // 2 :]:
        load.wait()
    get_table.wait()
    high, low = pick_rows(table_ref, 0, axis, groups), pick_rows(table_ref, 1, axis, groups)
    slots = [(outs[0], 0)] + [(outs[1 + s // 2], s % 2 * 2 * span if s > 1 else 0) for s in range(1, groups)]
    for (out, at), block in zip(slots, frame_blocks(groups, high, low, gather_rows(bs, 0, LANES))):
        for a in range(2):
            out[at + a * span : at + (a + 1) * span] = block[a]
    yt[:PAD] = zeros
    filter_rows(xs, yt, None, taps, rows - 16, 16, rows - 16)
    filter_rows(xs, yt, bt, taps, rows, 16, rows - 16)
    th, tl = split_value(gather_rows(bt, 16, 4))
    tail = dot_nt(th, high) + dot_nt(th, low) + dot_nt(tl, high)
    for step in [0, 1, *range(2, groups, 2)]:
        out, lanes = slots[step][0], step * span // LANES * LANES
        out[out.shape[0] - 8 :] = tail[:, lanes : lanes + LANES]


def coarse_rest_kernel(axis, groups, shares, table_ref, taps_ref, xs, *rest):
    lots = 2 + shares * (groups - 2)
    outs, (ys, bs) = rest[:lots], rest[lots:]
    small = 2 * LANES // (groups * shares)
    rows = xs.shape[0] - 2 * PAD
    taps = taps_ref[...]
    block = 64
    origin = rows // 2 - 16
    filter_rows(xs, ys, None, taps, origin, 16, origin)
    for base in range(rows // 2, rows, block):
        filter_rows(xs, ys, bs, taps, base, block, origin)
    high, low = pick_rows(table_ref, 0, axis, groups), pick_rows(table_ref, 1, axis, groups)
    for step, block in enumerate(frame_blocks(groups, high, low, gather_rows(bs, 16, LANES))):
        for share in range(shares):
            out, at = (outs[step], share * 2 * small) if step < 2 else (outs[share * (groups - 2) + step], 0)
            for a in range(2):
                out[at + a * small : at + (a + 1) * small] = block[a][share * small : (share + 1) * small]


def coarse_section(signal, coarse_taps, axis, groups, shares):
    length = signal.shape[1]
    taps_count, channels = coarse_taps.shape
    count = length // LANES
    rows = signal.reshape(2, count, LANES).transpose(1, 0, 2).reshape(2 * count, LANES)
    table = jnp.asarray(np.stack(split_table(coarse_table(channels, groups, shares))))
    span = 2 * LANES // groups
    lots = 1 + groups // 2
    first = pl.pallas_call(
        lambda *refs: coarse_kernel(axis, groups, *refs),
        out_shape=[pltpu.VMEM((2 * span + 8, LANES), F32)] * 2
        + [pltpu.VMEM((4 * span + 8, LANES), F32)] * (groups // 2 - 1)
        + [
            pltpu.VMEM((2, 2 * LANES, 2 * LANES), BF16),
            pltpu.VMEM((taps_count, LANES), F32),
            pltpu.VMEM((2 * count + 2 * PAD, LANES), F32),
        ],
        in_specs=[ANY] * 3,
        out_specs=[VMEM] * (lots + 3),
        scratch_shapes=[
            pltpu.VMEM((taps_count, channels), F32),
            pltpu.VMEM((count + PAD, LANES), F32),
            pltpu.VMEM((count, LANES), F32),
            pltpu.VMEM((PAD + 32, LANES), F32),
            pltpu.VMEM((32, LANES), F32),
            pltpu.SemaphoreType.DMA((PIECES + 2,)),
        ],
        compiler_params=PARAMS,
        cost_estimate=COST,
        name="coarse",
    )(in_hbm(rows), in_hbm(coarse_taps), in_hbm(table))
    second = pl.pallas_call(
        lambda *refs: coarse_rest_kernel(axis, groups, shares, *refs),
        out_shape=[pltpu.VMEM((2 * span, LANES), F32)] * 2
        + [pltpu.VMEM((2 * span // shares, LANES), F32)] * (shares * (groups - 2)),
        in_specs=[VMEM] * 3,
        out_specs=[VMEM] * (2 + shares * (groups - 2)),
        scratch_shapes=[
            pltpu.VMEM((count + 16 + PAD, LANES), F32),
            pltpu.VMEM((count + 16, LANES), F32),
        ],
        compiler_params=PARAMS,
        cost_estimate=COST,
        name="coarse_rest",
    )(*[in_vmem(value) for value in first[lots:]])
    return first[:lots], second


def terms(xs, taps, parity, m, a, rows):
    reach = [(g, m - 2 * g - parity) for g in range((m - parity) // 2, -1, -1)]
    height = rows.stop - rows.start
    return [xs[g, a, rows] * tiled(taps[j], height) for g, j in reach if j < len(taps)]


def tiled(tap, height):
    return tap[:height] if height <= 8 else jnp.concatenate([tap] * (height // 8), axis=0)


def fine_start_kernel(axis, groups, shares, taps_ref, *refs):
    pieces, (out_ref, xs) = refs[:groups], refs[groups:]
    span = 2 * LANES // groups
    small, per, frames = span // shares, span // (4 * shares), 2 * groups
    me = lax.axis_index(axis)
    for step in range(groups):
        for a in range(2):
            xs[me ^ step, a] = pieces[step][a * span : (a + 1) * span]
    for step in range(groups):
        tail = jnp.transpose(pieces[step][pieces[step].shape[0] - 8 :])
        at = step * span % LANES
        tail = tail[at : at + span]
        owner = (me ^ step) + 1
        for a in range(2):
            xs[owner, a, :, 0:4] = xs[owner, a, :, 0:4] + tail[:, 4 * a : 4 * a + 4]
    for a in range(2):
        for h in range(2):
            phase = 2 * a + h
            taps = [taps_ref[phase, j] for j in range(taps_ref.shape[1])]
            for share in range(shares):
                for part in range(2):
                    at = share * small + (2 * part + h) * per
                    for m in range(frames):
                        value = sum(terms(xs, taps, 0, m, a, slice(at, at + per)))
                        out_ref[share, phase, part, m * per : (m + 1) * per] = value


def fine_kernel(axis, groups, shares, share, taps_ref, table_ref, turn_ref, acc_ref, *refs):
    pieces, (out_hbm, xs, fs, yh, yl, zs, os, sem) = refs[:groups], refs[-8:]
    small = 2 * LANES // (groups * shares)
    per, frames = small // 4, 2 * groups
    me = lax.axis_index(axis)
    for step in range(groups):
        base = share * 2 * small if step < 2 else 0
        for a in range(2):
            xs[me ^ step, a] = pieces[step][base + a * small : base + (a + 1) * small]
    turns = 2 if per >= 16 else 1
    part_of = per // turns
    height = part_of * frames
    length = height * 4
    high, low = table_ref[0], table_ref[1]
    copies = [
        pltpu.make_async_copy(
            os.at[part, pl.ds(turn * length, length)],
            out_hbm.at[part, pl.ds((share * turns + turn) * length, length)],
            sem.at[2 * turn + part],
        )
        for turn in range(turns)
        for part in range(2)
    ]

    def run(turn):
        top = turn * 4 * height
        for a in range(2):
            for h in range(2):
                phase = 2 * a + h
                taps = [taps_ref[phase, j] for j in range(taps_ref.shape[1])]
                columns = []
                for part in range(2):
                    at = (2 * part + h) * per + turn * part_of
                    rows = slice(at, at + part_of)
                    for m in range(frames):
                        at = m * per + turn * part_of
                        value = sum(terms(xs, taps, 1, m, a, rows), acc_ref[share, phase, part, at : at + part_of])
                        at = m * part_of
                        fs[turn, phase, part, at : at + part_of] = value
                    picked = [fs[turn, phase, part, pl.ds(k, frames, stride=part_of), :] for k in range(part_of)]
                    columns.append(jnp.concatenate(picked, axis=0))
                first, second = split_value(jnp.concatenate(columns, axis=1))
                at = top + phase * height
                yh[at : at + height] = first
                yl[at : at + height] = second
        left, right = yh[top : top + 4 * height], yl[top : top + 4 * height]
        zs[top : top + 4 * height] = dot_nn(left, high) + dot_nn(right, high) + dot_nn(left, low)
        for at in range(0, height, 8):
            z = []
            for phase in range(4):
                row = top + phase * height + at
                real, imag = zs[row : row + 8, :LANES], zs[row : row + 8, LANES:]
                if phase:
                    c, s = turn_ref[phase, 0], turn_ref[phase, 1]
                    real, imag = real * c - imag * s, real * s + imag * c
                z.append((real, imag))
            (ar, ai), (br, bi), (cr, ci), (dr, di) = z
            pr, pi, qr, qi = ar + cr, ai + ci, ar - cr, ai - ci
            ur, ui, vr, vi = br + dr, bi + di, br - dr, bi - di
            reals = (pr + ur, qr + vi, pr - ur, qr - vi)
            imags = (pi + ui, qi - vr, pi - ui, qi + vr)
            for part, values in enumerate((reals, imags)):
                for r, value in enumerate(values):
                    row = turn * length + (at // 8 * 4 + r) * 8
                    os[part, row : row + 8, :] = value
        copies[2 * turn].start()
        copies[2 * turn + 1].start()

    run(0)
    for turn in range(1, turns):
        pl.when(me >= 0)(lambda turn=turn: run(turn))
    for copy in copies:
        copy.wait()


def tables_kernel(spread_hbm, table_hbm, turn_hbm, spread_ref, table_ref, turn_ref, taps_ref, sems):
    copies = [
        pltpu.make_async_copy(source, target, sems.at[i])
        for i, (source, target) in enumerate(((spread_hbm, taps_ref), (table_hbm, table_ref), (turn_hbm, turn_ref)))
    ]
    for copy in copies:
        copy.start()
    for copy in copies:
        copy.wait()
    for phase in range(taps_ref.shape[0]):
        for j in range(taps_ref.shape[1]):
            spread_ref[phase, j] = jnp.broadcast_to(taps_ref[phase, j : j + 1], (8, LANES))


def fine_tables_section(fine_taps):
    taps_count, fine = fine_taps.shape
    taps = fine_taps.reshape(taps_count, LANES, fine // LANES).transpose(2, 0, 1)
    table, turns = fine_tables(fine)
    turns = np.repeat(turns[:, :, None, :], 8, axis=2)
    shape = (fine // LANES, taps_count, 8, LANES)
    return pl.pallas_call(
        tables_kernel,
        out_shape=[
            pltpu.VMEM(shape, F32),
            pltpu.VMEM((2, 2 * LANES, 2 * LANES), BF16),
            pltpu.VMEM(turns.shape, F32),
        ],
        in_specs=[ANY] * 3,
        out_specs=[VMEM] * 3,
        scratch_shapes=[pltpu.VMEM(taps.shape, F32), pltpu.SemaphoreType.DMA((3,))],
        compiler_params=PARAMS,
        cost_estimate=COST,
        name="tables",
    )(taps, in_hbm(jnp.asarray(np.stack(split_table(table)))), in_hbm(jnp.asarray(turns)))


def fine_begin(pieces, taps, axis, groups, shares):
    span = 2 * LANES // groups
    per, frames = span // (4 * shares), 2 * groups
    acc = pl.pallas_call(
        lambda *refs: fine_start_kernel(axis, groups, shares, *refs),
        out_shape=pltpu.VMEM((shares, 4, 2, frames * per, LANES), F32),
        in_specs=[VMEM] * (1 + groups),
        out_specs=VMEM,
        scratch_shapes=[pltpu.VMEM((groups + 1, 2, span, LANES), F32)],
        compiler_params=PARAMS,
        cost_estimate=COST,
        name="fine_start",
    )(in_vmem(taps), *[in_vmem(value) for value in pieces])
    return acc


def fine_section(moved, tables, acc, axis, groups, shares):
    small = 2 * LANES // (groups * shares)
    per, frames = small // 4, 2 * groups
    height = 4 * frames * per
    length = per * frames * 4
    shared = [*tables, acc]
    out = None
    for share in range(shares):
        more = [] if out is None else [out]
        out = pl.pallas_call(
            lambda *refs: fine_kernel(axis, groups, shares, share, *refs),
            out_shape=pltpu.HBM((2, shares * length, LANES), F32),
            in_specs=[VMEM] * (4 + groups) + [ANY] * len(more),
            out_specs=ANY,
            scratch_shapes=[
                pltpu.VMEM((groups, 2, small, LANES), F32),
                pltpu.VMEM((2, 4, 2, frames * per, LANES), F32),
                pltpu.VMEM((height, 2 * LANES), BF16),
                pltpu.VMEM((height, 2 * LANES), BF16),
                pltpu.VMEM((height, 2 * LANES), F32),
                pltpu.VMEM((2, length, LANES), F32),
                pltpu.SemaphoreType.DMA((4,)),
            ],
            input_output_aliases={4 + groups: 0} if more else {},
            compiler_params=PARAMS,
            cost_estimate=COST,
            name="fine",
        )(*[in_vmem(value) for value in shared + list(moved[share])], *more)
    out = out.reshape(2, shares * per, frames // 8, 4, 8, LANES).transpose(0, 1, 2, 4, 3, 5)
    return out.reshape(2, shares * per, frames, 4 * LANES)


def solution(mesh):
    axis = "tm"
    groups = mesh.shape[axis]

    def swap(value, step):
        return lax.ppermute(value, axis, [(i, i ^ step) for i in range(groups)])

    def staged(signal, coarse_taps, fine_taps):
        shares = 1
        first, second = coarse_section(signal, coarse_taps, axis, groups, shares)
        reached = [swap(first[step // 2 + 1], step) for step in range(2, groups, 2)]
        pieces = [first[0], swap(first[1], 1)]
        moved = [
            [second[0], None]
            + [swap(second[share * (groups - 2) + step], step) for step in range(2, groups)]
            for share in range(shares)
        ]
        beside = swap(second[1], 1)
        for row in moved:
            row[1] = beside
        for value in reached:
            half = value[value.shape[0] // 2 - 4 :]
            pieces += [value, swap(half, 1)]
        tables = fine_tables_section(fine_taps)
        acc = fine_begin(pieces, tables[0], axis, groups, shares)
        return fine_section(moved, tables, acc, axis, groups, shares)

    return jax.shard_map(
        staged,
        mesh=mesh,
        in_specs=(P(None, ("streams", "tm")), P(), P()),
        out_specs=P(None, "tm", "streams", None),
        check_vma=False,
    )
```

time: 13.7 us -> 17.2 us (1.26)
  waiting for transfers between devices: 3.75 us -> 6.27 us
  Pallas kernels: 4.05 us -> 5.05 us
    ppermute x6, waiting for transfers between devices: 3.75 us -> 6.27 us  [swap(): return lax.ppermute(value, axis, [(i, i ^ step) for i in range(groups)])]
    pallas_call x3 -> x4, Pallas kernels: 2.39 us -> 3.38 us  [the longest x1 1.37 us: fine_section(): pl.pallas_call(lambda *refs: fine_kernel(axis, groups, shares, share, *re...]
  transfers between devices with their start and end apart: 6 -> 6, of which waited for: 3 -> 3; matrix products, arithmetic and copies ran while one was open for 2% -> 1% of each run, Pallas kernels for 7% -> 12%
where the time goes in v4:
time: 17.2 us; the launch traced here: 17 us
  waiting for transfers between devices  6.27 us (36%)
  starting transfers between devices  5.36 us (31%)
  Pallas kernels  5.05 us (29%)
  local copies, waits for them, and re-layouts  0.26 us (2%)
    ppermute x6, waiting for transfers between devices, swap(): return lax.ppermute(value, axis, [(i, i ^ step) for i in range(groups)])  6.27 us
    ppermute x6, starting transfers between devices, swap(): return lax.ppermute(value, axis, [(i, i ^ step) for i in range(groups)])  5.36 us
    pallas_call x1, Pallas kernels, coarse_section(): pl.pallas_call(lambda *refs: coarse_kernel(axis, groups, *refs), out_shap...  1.67 us
    pallas_call x1, Pallas kernels, fine_section(): pl.pallas_call(lambda *refs: fine_kernel(axis, groups, shares, share, *re...  1.37 us
    pallas_call x1, Pallas kernels, fine_tables_section(): pl.pallas_call(tables_kernel, out_shape=[pltpu.VMEM(shape, F32), pltpu.VM...  1.03 us
    pallas_call x1, Pallas kernels, coarse_section(): pl.pallas_call(lambda *refs: coarse_rest_kernel(axis, groups, shares, *re...  0.62 us
    pallas_call x1, Pallas kernels, fine_begin(): pl.pallas_call(lambda *refs: fine_start_kernel(axis, groups, shares, *ref...  0.36 us
  transfers between devices with their start and end apart: 6, of which 3 were waited for; matrix products, arithmetic and copies ran while one was open for 1% of the time, Pallas kernels for 12%

profile of v4, /device:TPU:0, one launch (start us, length us, event | category | flops | bytes accessed | tf_op | source)
XLA Modules:
  0.0 17.0 jit_solution(9497555591406694482)
XLA Ops:
  0.0 1.7 %coarse.1 = (f32[136,128]{1,0:T(8,128)S(1)}, f32[136,128]{1,0:T(8,128)S(1)}, f32[264,128]{1,0:T(8,128)S(1)}, bf16[2,256,256]{2,1,0:T(8,128)(2,1)S(1)}, f32[16,128]{1,0:T(8,128)S(1)}, /*index=5*/f32[1056,128]{1,0:T(8,128)S(1)}) custom-call(f32[1024,128]{1,0:T(8,128)} %bitcast.14, f32[16,64]{1,0:T(8,128)} %refs_1_.1, bf16[2,256,256]{2,1,0:T(8,128)(2,1)} %constant.6.clone.refs_2_), custom_call_target="tpu_custom_call" | custom-call | flops 2000000 | bytes 1000000 | tf_op jit(solution)/shard_map/coarse/pallas_call | solution.py:202
  1.7 3.1 %collective-permute-start.1 = (f32[264,128]{1,0:T(8,128)S(1)}, f32[264,128]{1,0:T(8,128)S(1)}, u32[]{:S(2)}, u32[]{:S(2)}) collective-permute-start(f32[264,128]{1,0:T(8,128)S(1)} %get-tuple-element.23), channel_id=1, source_target_pairs={{0,2},{1,3},{2,0},{3,1},{4,6},{5,7},{6,4},{7,5},{8,10},{9,11},{10,... | collective-permute-start | bytes 405512 | tf_op jit(solution)/shard_map/ppermute | solution.py:443
  4.7 0.0 collective-permute-start
  4.7 3.6 %collective-permute-done.1.refs_3_ = f32[264,128]{1,0:T(8,128)S(1)} collective-permute-done((f32[264,128]{1,0:T(8,128)S(1)}, f32[264,128]{1,0:T(8,128)S(1)}, u32[]{:S(2)}, u32[]{:S(2)}) %collective-permute-start.1) | collective-permute-done | bytes 135200 | tf_op jit(solution)/shard_map/ppermute | solution.py:443
  8.3 0.0 collective-permute-start.2
  8.3 0.0 copy-start
  8.3 0.6 %coarse_rest.1 = (f32[128,128]{1,0:T(8,128)S(1)}, f32[128,128]{1,0:T(8,128)S(1)}, f32[128,128]{1,0:T(8,128)S(1)}, f32[128,128]{1,0:T(8,128)S(1)}) custom-call(bf16[2,256,256]{2,1,0:T(8,128)(2,1)S(1)} %get-tuple-element.24.refs_0_, f32[16,128]{1,0:T(8,128)S(1)} %get-tuple-element.25.refs_1_, f32[1056,128]{1,0:T(8,128)S(1)} %get-tuple-element.26.refs_2_), custom_call_target="tpu_custom_call" | custom-call | flops 2000000 | bytes 1000000 | tf_op jit(solution)/shard_map/coarse_rest/pallas_call | solution.py:225
  9.0 0.5 %collective-permute-start.3 = (f32[128,128]{1,0:T(8,128)S(1)}, f32[128,128]{1,0:T(8,128)S(1)}, u32[]{:S(2)}, u32[]{:S(2)}) collective-permute-start(f32[128,128]{1,0:T(8,128)S(1)} %get-tuple-element.28), channel_id=1, source_target_pairs={{0,1},{1,0},{2,3},{3,2},{4,5},{5,4},{6,7},{7,6},{8,9},{9,8},{10,11... | collective-permute-start | bytes 196616 | tf_op jit(solution)/shard_map/ppermute | solution.py:443
  9.5 1.7 %collective-permute-start.4 = (f32[128,128]{1,0:T(8,128)S(1)}, f32[128,128]{1,0:T(8,128)S(1)}, u32[]{:S(2)}, u32[]{:S(2)}) collective-permute-start(f32[128,128]{1,0:T(8,128)S(1)} %get-tuple-element.29), channel_id=1, source_target_pairs={{0,2},{1,3},{2,0},{3,1},{4,6},{5,7},{6,4},{7,5},{8,10},{9,11},{10,... | collective-permute-start | bytes 196616 | tf_op jit(solution)/shard_map/ppermute | solution.py:443
  11.3 0.0 collective-permute-start.5
  11.3 0.0 copy-done
  11.3 0.1 copy.8
  11.4 0.1 copy.9
  11.5 1.0 %tables.1 = (f32[4,12,8,128]{3,2,1,0:T(8,128)S(1)}, bf16[2,256,256]{2,1,0:T(8,128)(2,1)S(1)}, f32[4,2,8,128]{3,2,1,0:T(8,128)S(1)}) custom-call(f32[4,12,128]{2,1,0:T(8,128)S(1)} %bitcast.12, bf16[2,256,256]{2,1,0:T(8,128)(2,1)} %constant.7.clone.table_hbm, f32[4,2,8,128]{3,2,1,0:T(8,128)} %constant.8.clone.turn_hbm), custom_call_target="tpu_custom_call" | custom-call | flops 2000000 | bytes 1000000 | tf_op jit(solution)/shard_map/tables/pallas_call | solution.py:374
  12.6 0.0 collective-permute-done.refs_2_
  12.6 0.0 collective-permute-done.2.refs_4_
  12.6 0.4 %fine_start.1.refs_3_ = f32[1,4,2,128,128]{4,3,2,1,0:T(8,128)S(1)} custom-call(f32[4,12,8,128]{3,2,1,0:T(8,128)S(1)} %get-tuple-element.18.refs_0_, f32[136,128]{1,0:T(8,128)S(1)} %get-tuple-element.21.refs_1_, f32[136,128]{1,0:T(8,128)S(1)} %collective-permute-done.refs_2_, f32[264,128]{1,0:T(8,128)S(1)} %collective-permute-done.1.refs_3_, ...), custom_call_target="tpu_custom_call" | custom-call | flops 2000000 | bytes 1000000 | tf_op jit(solution)/shard_map/fine_start/pallas_call | solution.py:393
  12.9 0.0 collective-permute-done.3.refs_5_
  13.0 0.8 %collective-permute-done.4.refs_6_ = f32[128,128]{1,0:T(8,128)S(1)} collective-permute-done((f32[128,128]{1,0:T(8,128)S(1)}, f32[128,128]{1,0:T(8,128)S(1)}, u32[]{:S(2)}, u32[]{:S(2)}) %collective-permute-start.4) | collective-permute-done | bytes 65568 | tf_op jit(solution)/shard_map/ppermute | solution.py:443
  13.8 1.9 %collective-permute-done.5.refs_7_ = f32[128,128]{1,0:T(8,128)S(1)} collective-permute-done((f32[128,128]{1,0:T(8,128)S(1)}, f32[128,128]{1,0:T(8,128)S(1)}, u32[]{:S(2)}, u32[]{:S(2)}) %collective-permute-start.5) | collective-permute-done | bytes 65568 | tf_op jit(solution)/shard_map/ppermute | solution.py:443
  15.6 1.4 %fine.1 = f32[2,512,128]{2,1,0:T(8,128)} custom-call(f32[4,12,8,128]{3,2,1,0:T(8,128)S(1)} %get-tuple-element.18.refs_0_, bf16[2,256,256]{2,1,0:T(8,128)(2,1)S(1)} %get-tuple-element.19.refs_1_, f32[4,2,8,128]{3,2,1,0:T(8,128)S(1)} %get-tuple-element.20.refs_2_, f32[1,4,2,128,128]{4,3,2,1,0:T(8,128)S(1)} %fine_start.1.refs_3_, ...), custom_call_target="tpu_custom_call" | custom-call | flops 2000000 | bytes 1000000 | tf_op jit(solution)/shard_map/fine/pallas_call | solution.py:415
  (1 shorter events, 0.0 us)
Async XLA Ops:
  1.7 6.6 %collective-permute-start.1 = (f32[264,128]{1,0:T(8,128)S(1)}, f32[264,128]{1,0:T(8,128)S(1)}, u32[]{:S(2)}, u32[]{:S(2)}) collective-permute-start(f32[264,128]{1,0:T(8,128)S(1)} %get-tuple-element.23), channel_id=1, source_target_pairs={{0,2},{1,3},{2,0},{3,1},{4,6},{5,7},{6,4},{7,5},{8,10},{9,11},{10,... | collective-permute-start | bytes 405512 | tf_op jit(solution)/shard_map/ppermute | solution.py:443
  4.7 7.8 %collective-permute-start = (f32[136,128]{1,0:T(8,128)S(1)}, f32[136,128]{1,0:T(8,128)S(1)}, u32[]{:S(2)}, u32[]{:S(2)}) collective-permute-start(f32[136,128]{1,0:T(8,128)S(1)} %get-tuple-element.22), channel_id=1, source_target_pairs={{0,1},{1,0},{2,3},{3,2},{4,5},{5,4},{6,7},{7,6},{8,9},{9,8},{10,11... | collective-permute-start | bytes 208904 | tf_op jit(solution)/shard_map/ppermute | solution.py:443
  8.3 4.2 %collective-permute-start.2 = (f32[136,128]{1,0:T(8,128)S(1)}, f32[136,128]{1,0:T(8,128)S(1)}, u32[]{:S(2)}, u32[]{:S(2)}) collective-permute-start(f32[136,128]{1,0:T(8,128)S(1)} %slice.4), channel_id=1, source_target_pairs={{0,1},{1,0},{2,3},{3,2},{4,5},{5,4},{6,7},{7,6},{8,9},{9,8},{10,11... | collective-permute-start | bytes 208904 | tf_op jit(solution)/shard_map/ppermute | solution.py:443
  8.3 2.9 %copy-start = (f32[12,512]{1,0:T(8,128)S(1)}, f32[12,512]{1,0:T(8,128)}, u32[]{:S(2)}) copy-start(f32[12,512]{1,0:T(8,128)} %param.8) | copy-start | bytes 73732
  9.0 4.0 %collective-permute-start.3 = (f32[128,128]{1,0:T(8,128)S(1)}, f32[128,128]{1,0:T(8,128)S(1)}, u32[]{:S(2)}, u32[]{:S(2)}) collective-permute-start(f32[128,128]{1,0:T(8,128)S(1)} %get-tuple-element.28), channel_id=1, source_target_pairs={{0,1},{1,0},{2,3},{3,2},{4,5},{5,4},{6,7},{7,6},{8,9},{9,8},{10,11... | collective-permute-start | bytes 196616 | tf_op jit(solution)/shard_map/ppermute | solution.py:443
  9.5 4.3 %collective-permute-start.4 = (f32[128,128]{1,0:T(8,128)S(1)}, f32[128,128]{1,0:T(8,128)S(1)}, u32[]{:S(2)}, u32[]{:S(2)}) collective-permute-start(f32[128,128]{1,0:T(8,128)S(1)} %get-tuple-element.29), channel_id=1, source_target_pairs={{0,2},{1,3},{2,0},{3,1},{4,6},{5,7},{6,4},{7,5},{8,10},{9,11},{10,... | collective-permute-start | bytes 196616 | tf_op jit(solution)/shard_map/ppermute | solution.py:443
  11.3 4.4 %collective-permute-start.5 = (f32[128,128]{1,0:T(8,128)S(1)}, f32[128,128]{1,0:T(8,128)S(1)}, u32[]{:S(2)}, u32[]{:S(2)}) collective-permute-start(f32[128,128]{1,0:T(8,128)S(1)} %get-tuple-element.30), channel_id=1, source_target_pairs={{0,3},{1,2},{2,1},{3,0},{4,7},{5,6},{6,5},{7,4},{8,11},{9,10},{10,... | collective-permute-start | bytes 196616 | tf_op jit(solution)/shard_map/ppermute | solution.py:443

commit v5 on v4

--- a/solution.py
+++ b/solution.py
@@ -77,10 +77,10 @@
     return pltpu.with_memory_space_constraint(value, pltpu.HBM)
 
 
-def pick_rows(table_ref, half, axis, groups):
+def pick_rows(table_ref, half, axis, groups, steps):
     me = lax.axis_index(axis)
     span = 2 * LANES // groups
-    picks = [pl.multiple_of((me ^ step) * span, span) for step in range(groups)]
+    picks = [pl.multiple_of((me ^ step) * span, span) for step in steps]
     return jnp.concatenate([table_ref[half, pl.ds(pick, span), :] for pick in picks], axis=0)
 
 
@@ -113,19 +113,23 @@
     return jnp.concatenate(parts, axis=0)
 
 
-def frame_blocks(groups, high, low, gathered):
-    span = 2 * LANES // groups
-    bh, bl = split_value(gathered)
+def frame_blocks(span, high, low, bh, bl):
     result = dot_nt(high, bh) + dot_nt(low, bh) + dot_nt(high, bl)
     return [
-        [result[step * span : (step + 1) * span, a * LANES : (a + 1) * LANES] for a in range(2)]
-        for step in range(groups)
+        [result[at : at + span, a * LANES : (a + 1) * LANES] for a in range(2)]
+        for at in range(0, high.shape[0], span)
     ]
 
 
+def tail_rows(high, low, th, tl):
+    tail = dot_nt(th, high) + dot_nt(th, low) + dot_nt(tl, high)
+    spare = -tail.shape[1] % LANES
+    return jnp.concatenate([tail, jnp.zeros((tail.shape[0], spare), F32)], axis=1) if spare else tail
+
+
 def coarse_kernel(axis, groups, x_hbm, taps_hbm, table_hbm, *rest):
-    lots = 1 + groups // 2
-    outs, (table_ref, taps_out, xs, taps_ref, ys, bs, yt, bt, sems) = rest[:lots], rest[lots:]
+    lots = groups // 2 - 1
+    outs, (bh_ref, bl_ref, th_ref, tl_ref, table_ref, taps_out, xs, taps_ref, ys, bs, xt, yt, bt, sems) = rest[:lots], rest[lots:]
     rows = x_hbm.shape[0]
     span = 2 * LANES // groups
     step = rows // PIECES
@@ -135,10 +139,13 @@
     ]
     get_taps = pltpu.make_async_copy(taps_hbm, taps_ref, sems.at[PIECES])
     get_table = pltpu.make_async_copy(table_hbm, table_ref, sems.at[PIECES + 1])
+    ends = 64
+    get_ends = pltpu.make_async_copy(x_hbm.at[pl.ds(rows - ends, ends)], xt.at[pl.ds(PAD, ends)], sems.at[PIECES + 2])
     get_taps.start()
     for load in loads[: PIECES // 2]:
         load.start()
     get_table.start()
+    get_ends.start()
     for load in loads[PIECES // 2 :]:
         load.start()
     zeros = jnp.zeros((PAD, LANES), F32)
@@ -154,28 +161,34 @@
         loads[i].wait()
         for base in range(i * step, (i + 1) * step, block):
             filter_rows(xs, ys, bs, taps, base, block, 0)
+    get_table.wait()
+    get_ends.wait()
+    steps = range(2, groups)
+    high, low = [pick_rows(table_ref, half, axis, groups, steps) for half in range(2)]
+    bh, bl = split_value(gather_rows(bs, 0, LANES))
+    bh_ref[...], bl_ref[...] = bh, bl
+    for i, block in enumerate(frame_blocks(span, high, low, bh, bl)):
+        for a in range(2):
+            at = i % 2 * 2 * span + a * span
+            outs[i // 2][at : at + span] = block[a]
+    yt[:PAD] = zeros
+    xt[PAD + ends :] = zeros
+    filter_rows(xt, yt, None, taps, ends - 16, 16, ends - 16)
+    filter_rows(xt, yt, bt, taps, ends, 16, ends - 16)
+    th, tl = split_value(jnp.concatenate([gather_rows(bt, 16, 4), jnp.zeros((8, 2 * LANES), F32)], axis=0))
+    th_ref[...], tl_ref[...] = th, tl
+    tail = tail_rows(high, low, th, tl)
+    for i, out in enumerate(outs):
+        lanes = 2 * i * span // LANES * LANES
+        out[4 * span :] = tail[:8, lanes : lanes + LANES]
     for load in loads[PIECES // 2 :]:
         load.wait()
-    get_table.wait()
-    high, low = pick_rows(table_ref, 0, axis, groups), pick_rows(table_ref, 1, axis, groups)
-    slots = [(outs[0], 0)] + [(outs[1 + s // 2], s % 2 * 2 * span if s > 1 else 0) for s in range(1, groups)]
-    for (out, at), block in zip(slots, frame_blocks(groups, high, low, gather_rows(bs, 0, LANES))):
-        for a in range(2):
-            out[at + a * span : at + (a + 1) * span] = block[a]
-    yt[:PAD] = zeros
-    filter_rows(xs, yt, None, taps, rows - 16, 16, rows - 16)
-    filter_rows(xs, yt, bt, taps, rows, 16, rows - 16)
-    th, tl = split_value(gather_rows(bt, 16, 4))
-    tail = dot_nt(th, high) + dot_nt(th, low) + dot_nt(tl, high)
-    for step in [0, 1, *range(2, groups, 2)]:
-        out, lanes = slots[step][0], step * span // LANES * LANES
-        out[out.shape[0] - 8 :] = tail[:, lanes : lanes + LANES]
-
-
-def coarse_rest_kernel(axis, groups, shares, table_ref, taps_ref, xs, *rest):
-    lots = 2 + shares * (groups - 2)
+
+
+def coarse_rest_kernel(axis, groups, bh_ref, bl_ref, th_ref, tl_ref, table_ref, taps_ref, xs, *rest):
+    lots = 1 + groups
     outs, (ys, bs) = rest[:lots], rest[lots:]
-    small = 2 * LANES // (groups * shares)
+    span = 2 * LANES // groups
     rows = xs.shape[0] - 2 * PAD
     taps = taps_ref[...]
     block = 64
@@ -183,12 +196,18 @@
     filter_rows(xs, ys, None, taps, origin, 16, origin)
     for base in range(rows // 2, rows, block):
         filter_rows(xs, ys, bs, taps, base, block, origin)
-    high, low = pick_rows(table_ref, 0, axis, groups), pick_rows(table_ref, 1, axis, groups)
-    for step, block in enumerate(frame_blocks(groups, high, low, gather_rows(bs, 16, LANES))):
-        for share in range(shares):
-            out, at = (outs[step], share * 2 * small) if step < 2 else (outs[share * (groups - 2) + step], 0)
-            for a in range(2):
-                out[at + a * small : at + (a + 1) * small] = block[a][share * small : (share + 1) * small]
+    high, low = [pick_rows(table_ref, half, axis, groups, range(groups)) for half in range(2)]
+    bh, bl = split_value(gather_rows(bs, 16, LANES))
+    for step, block in enumerate(frame_blocks(span, high, low, bh, bl)):
+        out, at = (outs[1 + step], 0) if step != 1 else (outs[2], 2 * span)
+        for a in range(2):
+            out[at + a * span : at + (a + 1) * span] = block[a]
+    near_high, near_low = high[: 2 * span], low[: 2 * span]
+    tail = tail_rows(near_high, near_low, th_ref[...], tl_ref[...])
+    for out, block in zip((outs[0], outs[2]), frame_blocks(span, near_high, near_low, bh_ref[...], bl_ref[...])):
+        for a in range(2):
+            out[a * span : (a + 1) * span] = block[a]
+        out[out.shape[0] - 8 :] = tail[:8, :LANES]
 
 
 def coarse_section(signal, coarse_taps, axis, groups, shares):
@@ -198,36 +217,38 @@
     rows = signal.reshape(2, count, LANES).transpose(1, 0, 2).reshape(2 * count, LANES)
     table = jnp.asarray(np.stack(split_table(coarse_table(channels, groups, shares))))
     span = 2 * LANES // groups
-    lots = 1 + groups // 2
+    lots = groups // 2 - 1
     first = pl.pallas_call(
         lambda *refs: coarse_kernel(axis, groups, *refs),
-        out_shape=[pltpu.VMEM((2 * span + 8, LANES), F32)] * 2
-        + [pltpu.VMEM((4 * span + 8, LANES), F32)] * (groups // 2 - 1)
+        out_shape=[pltpu.VMEM((4 * span + 8, LANES), F32)] * lots
+        + [pltpu.VMEM((2 * LANES, 2 * LANES), BF16)] * 2
+        + [pltpu.VMEM((16, 2 * LANES), BF16)] * 2
         + [
             pltpu.VMEM((2, 2 * LANES, 2 * LANES), BF16),
             pltpu.VMEM((taps_count, LANES), F32),
             pltpu.VMEM((2 * count + 2 * PAD, LANES), F32),
         ],
         in_specs=[ANY] * 3,
-        out_specs=[VMEM] * (lots + 3),
+        out_specs=[VMEM] * (lots + 7),
         scratch_shapes=[
             pltpu.VMEM((taps_count, channels), F32),
             pltpu.VMEM((count + PAD, LANES), F32),
             pltpu.VMEM((count, LANES), F32),
+            pltpu.VMEM((64 + 2 * PAD, LANES), F32),
             pltpu.VMEM((PAD + 32, LANES), F32),
             pltpu.VMEM((32, LANES), F32),
-            pltpu.SemaphoreType.DMA((PIECES + 2,)),
+            pltpu.SemaphoreType.DMA((PIECES + 3,)),
         ],
         compiler_params=PARAMS,
         cost_estimate=COST,
         name="coarse",
     )(in_hbm(rows), in_hbm(coarse_taps), in_hbm(table))
+    own, pair, late = [pltpu.VMEM((n * span + m, LANES), F32) for n, m in ((2, 8), (4, 8), (2, 0))]
     second = pl.pallas_call(
-        lambda *refs: coarse_rest_kernel(axis, groups, shares, *refs),
-        out_shape=[pltpu.VMEM((2 * span, LANES), F32)] * 2
-        + [pltpu.VMEM((2 * span // shares, LANES), F32)] * (shares * (groups - 2)),
-        in_specs=[VMEM] * 3,
-        out_specs=[VMEM] * (2 + shares * (groups - 2)),
+        lambda *refs: coarse_rest_kernel(axis, groups, *refs),
+        out_shape=[own, late, pair] + [late] * (groups - 2),
+        in_specs=[VMEM] * 7,
+        out_specs=[VMEM] * (1 + groups),
         scratch_shapes=[
             pltpu.VMEM((count + 16 + PAD, LANES), F32),
             pltpu.VMEM((count + 16, LANES), F32),
@@ -259,7 +280,7 @@
             xs[me ^ step, a] = pieces[step][a * span : (a + 1) * span]
     for step in range(groups):
         tail = jnp.transpose(pieces[step][pieces[step].shape[0] - 8 :])
-        at = step * span % LANES
+        at = (step - 2 if step > 1 else step) * span % LANES
         tail = tail[at : at + span]
         owner = (me ^ step) + 1
         for a in range(2):
@@ -282,7 +303,7 @@
     per, frames = small // 4, 2 * groups
     me = lax.axis_index(axis)
     for step in range(groups):
-        base = share * 2 * small if step < 2 else 0
+        base = 2 * small if step == 1 else 0
         for a in range(2):
             xs[me ^ step, a] = pieces[step][base + a * small : base + (a + 1) * small]
     turns = 2 if per >= 16 else 1
@@ -346,7 +367,7 @@
 
     run(0)
     for turn in range(1, turns):
-        pl.when(me >= 0)(lambda turn=turn: run(turn))
+        run(turn)
     for copy in copies:
         copy.wait()
 
@@ -445,16 +466,11 @@
     def staged(signal, coarse_taps, fine_taps):
         shares = 1
         first, second = coarse_section(signal, coarse_taps, axis, groups, shares)
-        reached = [swap(first[step // 2 + 1], step) for step in range(2, groups, 2)]
-        pieces = [first[0], swap(first[1], 1)]
-        moved = [
-            [second[0], None]
-            + [swap(second[share * (groups - 2) + step], step) for step in range(2, groups)]
-            for share in range(shares)
-        ]
-        beside = swap(second[1], 1)
-        for row in moved:
-            row[1] = beside
+        reached = [swap(value, 2 * i + 2) for i, value in enumerate(first)]
+        late = [swap(second[1 + step], step) for step in range(2, groups)]
+        beside = swap(second[2], 1)
+        moved = [[second[1], beside] + late]
+        pieces = [second[0], beside]
         for value in reached:
             half = value[value.shape[0] // 2 - 4 :]
             pieces += [value, swap(half, 1)]

time: 17.2 us -> 15.7 us (0.913)
  waiting for transfers between devices: 6.27 us -> 5.13 us
  starting transfers between devices: 5.36 us -> 4.99 us
    ppermute x6 -> x5, waiting for transfers between devices: 6.27 us -> 5.13 us  [swap(): return lax.ppermute(value, axis, [(i, i ^ step) for i in range(groups)])]
    ppermute x6 -> x5, starting transfers between devices: 5.36 us -> 4.99 us  [swap(): return lax.ppermute(value, axis, [(i, i ^ step) for i in range(groups)])]
  transfers between devices with their start and end apart: 6 -> 5, of which waited for: 3 -> 3; matrix products, arithmetic and copies ran while one was open for 1% -> 2% of each run, Pallas kernels for 12% -> 13%
where the time goes in v5:
time: 15.7 us; the launch traced here: 15.5 us
  waiting for transfers between devices  5.13 us (33%)
  Pallas kernels  5.04 us (32%)
  starting transfers between devices  4.99 us (32%)
  local copies, waits for them, and re-layouts  0.25 us (2%)
    ppermute x5, waiting for transfers between devices, swap(): return lax.ppermute(value, axis, [(i, i ^ step) for i in range(groups)])  5.13 us
    ppermute x5, starting transfers between devices, swap(): return lax.ppermute(value, axis, [(i, i ^ step) for i in range(groups)])  4.99 us
    pallas_call x1, Pallas kernels, coarse_section(): pl.pallas_call(lambda *refs: coarse_kernel(axis, groups, *refs), out_shap...  1.6 us
    pallas_call x1, Pallas kernels, fine_section(): pl.pallas_call(lambda *refs: fine_kernel(axis, groups, shares, share, *re...  1.36 us
    pallas_call x1, Pallas kernels, fine_tables_section(): pl.pallas_call(tables_kernel, out_shape=[pltpu.VMEM(shape, F32), pltpu.VM...  1.03 us
    pallas_call x1, Pallas kernels, coarse_section(): pl.pallas_call(lambda *refs: coarse_rest_kernel(axis, groups, *refs), out...  0.69 us
    pallas_call x1, Pallas kernels, fine_begin(): pl.pallas_call(lambda *refs: fine_start_kernel(axis, groups, shares, *ref...  0.36 us
  transfers between devices with their start and end apart: 5, of which 3 were waited for; matrix products, arithmetic and copies ran while one was open for 2% of the time, Pallas kernels for 13%

profile of v5, /device:TPU:0, one launch (start us, length us, event | category | flops | bytes accessed | tf_op | source)
XLA Modules:
  0.0 15.5 jit_solution(16955348268478813584)
XLA Ops:
  0.0 1.6 %coarse.1 = (f32[264,128]{1,0:T(8,128)S(1)}, bf16[256,256]{1,0:T(8,128)(2,1)S(1)}, bf16[256,256]{1,0:T(8,128)(2,1)S(1)}, bf16[16,256]{1,0:T(8,128)(2,1)S(1)}, bf...) custom-call(f32[1024,128]{1,0:T(8,128)} %bitcast.14, ...), custom_call_target="tpu_custom_call" | custom-call | flops 2000000 | bytes 1000000 | tf_op jit(solution)/shard_map/coarse/pallas_call | solution.py:221
  1.6 3.1 %collective-permute-start.1 = (f32[264,128]{1,0:T(8,128)S(1)}, f32[264,128]{1,0:T(8,128)S(1)}, u32[]{:S(2)}, u32[]{:S(2)}) collective-permute-start(f32[264,128]{1,0:T(8,128)S(1)} %get-tuple-element.33), channel_id=1, source_target_pairs={{0,2},{1,3},{2,0},{3,1},{4,6},{5,7},{6,4},{7,5},{8,10},{9,11},{10,... | collective-permute-start | bytes 405512 | tf_op jit(solution)/shard_map/ppermute | solution.py:464
  4.7 0.7 %coarse_rest.1 = (f32[136,128]{1,0:T(8,128)S(1)}, f32[128,128]{1,0:T(8,128)S(1)}, f32[264,128]{1,0:T(8,128)S(1)}, f32[128,128]{1,0:T(8,128)S(1)}, f32[128,128]{1,0:T(8,128)S(1)}) custom-call(bf16[256,256]{1,0:T(8,128)(2,1)S(1)} %get-tuple-element.24.refs_0_, bf16[256,256]{1,0:T(8,128)(2,1)S(1)} %get-tuple-element.25.refs_1_, ...), custom_call_target="tpu_custom_call" | custom-call | flops 2000000 | bytes 1000000 | tf_op jit(solution)/shard_map/coarse_rest/pallas_call | solution.py:247
  5.4 0.0 copy-start
  5.4 0.1 collective-permute-start
  5.5 2.8 %collective-permute-done.1.refs_3_ = f32[264,128]{1,0:T(8,128)S(1)} collective-permute-done((f32[264,128]{1,0:T(8,128)S(1)}, f32[264,128]{1,0:T(8,128)S(1)}, u32[]{:S(2)}, u32[]{:S(2)}) %collective-permute-start.1) | collective-permute-done | bytes 135200 | tf_op jit(solution)/shard_map/ppermute | solution.py:464
  8.3 0.0 collective-permute-start.2
  8.3 1.8 %collective-permute-start.3 = (f32[128,128]{1,0:T(8,128)S(1)}, f32[128,128]{1,0:T(8,128)S(1)}, u32[]{:S(2)}, u32[]{:S(2)}) collective-permute-start(f32[128,128]{1,0:T(8,128)S(1)} %get-tuple-element.35), channel_id=1, source_target_pairs={{0,2},{1,3},{2,0},{3,1},{4,6},{5,7},{6,4},{7,5},{8,10},{9,11},{10,... | collective-permute-start | bytes 196616 | tf_op jit(solution)/shard_map/ppermute | solution.py:464
  10.1 0.0 collective-permute-start.4
  10.1 0.0 copy-done
  10.1 0.1 copy.8
  10.3 0.1 copy.9
  10.4 1.0 %tables.1 = (f32[4,12,8,128]{3,2,1,0:T(8,128)S(1)}, bf16[2,256,256]{2,1,0:T(8,128)(2,1)S(1)}, f32[4,2,8,128]{3,2,1,0:T(8,128)S(1)}) custom-call(f32[4,12,128]{2,1,0:T(8,128)S(1)} %bitcast.12, bf16[2,256,256]{2,1,0:T(8,128)(2,1)} %constant.7.clone.table_hbm, f32[4,2,8,128]{3,2,1,0:T(8,128)} %constant.8.clone.turn_hbm), custom_call_target="tpu_custom_call" | custom-call | flops 2000000 | bytes 1000000 | tf_op jit(solution)/shard_map/tables/pallas_call | solution.py:395
  11.4 0.0 collective-permute-done.refs_2_.refs_5_
  11.4 0.0 collective-permute-done.2.refs_4_
  11.4 0.4 %fine_start.1.refs_3_ = f32[1,4,2,128,128]{4,3,2,1,0:T(8,128)S(1)} custom-call(f32[4,12,8,128]{3,2,1,0:T(8,128)S(1)} %get-tuple-element.21.refs_0_, f32[136,128]{1,0:T(8,128)S(1)} %get-tuple-element.31.refs_1_, f32[264,128]{1,0:T(8,128)S(1)} %collective-permute-done.refs_2_.refs_5_, f32[264,128]{1,0:T(8,128)S(1)} %collective-permute-done.1.refs_3_, ...), custom_call_target="tpu_custom_call" | custom-call | flops 2000000 | bytes 1000000 | tf_op jit(solution)/shard_map/fine_start/pallas_call | solution.py:414
  11.8 1.0 %collective-permute-done.3.refs_6_ = f32[128,128]{1,0:T(8,128)S(1)} collective-permute-done((f32[128,128]{1,0:T(8,128)S(1)}, f32[128,128]{1,0:T(8,128)S(1)}, u32[]{:S(2)}, u32[]{:S(2)}) %collective-permute-start.3) | collective-permute-done | bytes 65568 | tf_op jit(solution)/shard_map/ppermute | solution.py:464
  12.8 1.4 %collective-permute-done.4.refs_7_ = f32[128,128]{1,0:T(8,128)S(1)} collective-permute-done((f32[128,128]{1,0:T(8,128)S(1)}, f32[128,128]{1,0:T(8,128)S(1)}, u32[]{:S(2)}, u32[]{:S(2)}) %collective-permute-start.4) | collective-permute-done | bytes 65568 | tf_op jit(solution)/shard_map/ppermute | solution.py:464
  14.1 1.4 %fine.1 = f32[2,512,128]{2,1,0:T(8,128)} custom-call(f32[4,12,8,128]{3,2,1,0:T(8,128)S(1)} %get-tuple-element.21.refs_0_, bf16[2,256,256]{2,1,0:T(8,128)(2,1)S(1)} %get-tuple-element.22.refs_1_, f32[4,2,8,128]{3,2,1,0:T(8,128)S(1)} %get-tuple-element.23.refs_2_, f32[1,4,2,128,128]{4,3,2,1,0:T(8,128)S(1)} %fine_start.1.refs_3_, ...), custom_call_target="tpu_custom_call" | custom-call | flops 2000000 | bytes 1000000 | tf_op jit(solution)/shard_map/fine/pallas_call | solution.py:436
  (1 shorter events, 0.0 us)
Async XLA Ops:
  1.6 6.6 %collective-permute-start.1 = (f32[264,128]{1,0:T(8,128)S(1)}, f32[264,128]{1,0:T(8,128)S(1)}, u32[]{:S(2)}, u32[]{:S(2)}) collective-permute-start(f32[264,128]{1,0:T(8,128)S(1)} %get-tuple-element.33), channel_id=1, source_target_pairs={{0,2},{1,3},{2,0},{3,1},{4,6},{5,7},{6,4},{7,5},{8,10},{9,11},{10,... | collective-permute-start | bytes 405512 | tf_op jit(solution)/shard_map/ppermute | solution.py:464
  5.4 4.8 %copy-start = (f32[12,512]{1,0:T(8,128)S(1)}, f32[12,512]{1,0:T(8,128)}, u32[]{:S(2)}) copy-start(f32[12,512]{1,0:T(8,128)} %param.8) | copy-start | bytes 73732
  5.4 6.0 %collective-permute-start = (f32[264,128]{1,0:T(8,128)S(1)}, f32[264,128]{1,0:T(8,128)S(1)}, u32[]{:S(2)}, u32[]{:S(2)}) collective-permute-start(f32[264,128]{1,0:T(8,128)S(1)} %get-tuple-element.32), channel_id=1, source_target_pairs={{0,1},{1,0},{2,3},{3,2},{4,5},{5,4},{6,7},{7,6},{8,9},{9,8},{10,11... | collective-permute-start | bytes 405512 | tf_op jit(solution)/shard_map/ppermute | solution.py:464
  8.3 3.2 %collective-permute-start.2 = (f32[136,128]{1,0:T(8,128)S(1)}, f32[136,128]{1,0:T(8,128)S(1)}, u32[]{:S(2)}, u32[]{:S(2)}) collective-permute-start(f32[136,128]{1,0:T(8,128)S(1)} %slice.4), channel_id=1, source_target_pairs={{0,1},{1,0},{2,3},{3,2},{4,5},{5,4},{6,7},{7,6},{8,9},{9,8},{10,11... | collective-permute-start | bytes 208904 | tf_op jit(solution)/shard_map/ppermute | solution.py:464
  8.3 4.5 %collective-permute-start.3 = (f32[128,128]{1,0:T(8,128)S(1)}, f32[128,128]{1,0:T(8,128)S(1)}, u32[]{:S(2)}, u32[]{:S(2)}) collective-permute-start(f32[128,128]{1,0:T(8,128)S(1)} %get-tuple-element.35), channel_id=1, source_target_pairs={{0,2},{1,3},{2,0},{3,1},{4,6},{5,7},{6,4},{7,5},{8,10},{9,11},{10,... | collective-permute-start | bytes 196616 | tf_op jit(solution)/shard_map/ppermute | solution.py:464
  10.1 4.1 %collective-permute-start.4 = (f32[128,128]{1,0:T(8,128)S(1)}, f32[128,128]{1,0:T(8,128)S(1)}, u32[]{:S(2)}, u32[]{:S(2)}) collective-permute-start(f32[128,128]{1,0:T(8,128)S(1)} %get-tuple-element.36), channel_id=1, source_target_pairs={{0,3},{1,2},{2,1},{3,0},{4,7},{5,6},{6,5},{7,4},{8,11},{9,10},{10,... | collective-permute-start | bytes 196616 | tf_op jit(solution)/shard_map/ppermute | solution.py:464

commit v6 on v5

--- a/solution.py
+++ b/solution.py
@@ -270,21 +270,24 @@
     return tap[:height] if height <= 8 else jnp.concatenate([tap] * (height // 8), axis=0)
 
 
-def fine_start_kernel(axis, groups, shares, taps_ref, *refs):
-    pieces, (out_ref, xs) = refs[:groups], refs[groups:]
+def add_piece(axis, groups, piece, step, xs):
+    span = 2 * LANES // groups
+    owner = lax.axis_index(axis) ^ step
+    at = (step - 2 if step > 1 else step) * span % LANES
+    tail = jnp.transpose(piece[piece.shape[0] - 8 :])[at : at + span]
+    for a in range(2):
+        xs[owner, a] = xs[owner, a] + piece[a * span : (a + 1) * span]
+        xs[owner + 1, a, :, 0:4] = xs[owner + 1, a, :, 0:4] + tail[:, 4 * a : 4 * a + 4]
+
+
+def fine_start_kernel(axis, groups, shares, taps_ref, near_ref, *refs):
+    steps = range(3, groups, 2)
+    pieces, (out_ref, xs) = refs[: len(steps)], refs[len(steps) :]
     span = 2 * LANES // groups
     small, per, frames = span // shares, span // (4 * shares), 2 * groups
-    me = lax.axis_index(axis)
-    for step in range(groups):
-        for a in range(2):
-            xs[me ^ step, a] = pieces[step][a * span : (a + 1) * span]
-    for step in range(groups):
-        tail = jnp.transpose(pieces[step][pieces[step].shape[0] - 8 :])
-        at = (step - 2 if step > 1 else step) * span % LANES
-        tail = tail[at : at + span]
-        owner = (me ^ step) + 1
-        for a in range(2):
-            xs[owner, a, :, 0:4] = xs[owner, a, :, 0:4] + tail[:, 4 * a : 4 * a + 4]
+    xs[...] = near_ref[...]
+    for step, piece in zip(steps, pieces):
+        add_piece(axis, groups, piece, step, xs)
     for a in range(2):
         for h in range(2):
             phase = 2 * a + h
@@ -372,13 +375,18 @@
         copy.wait()
 
 
-def tables_kernel(spread_hbm, table_hbm, turn_hbm, spread_ref, table_ref, turn_ref, taps_ref, sems):
+def tables_kernel(axis, groups, spread_hbm, table_hbm, turn_hbm, *refs):
+    steps = [0, 1, *range(2, groups, 2)]
+    pieces, (spread_ref, table_ref, turn_ref, near_ref, taps_ref, sems) = refs[: len(steps)], refs[len(steps) :]
     copies = [
         pltpu.make_async_copy(source, target, sems.at[i])
         for i, (source, target) in enumerate(((spread_hbm, taps_ref), (table_hbm, table_ref), (turn_hbm, turn_ref)))
     ]
     for copy in copies:
         copy.start()
+    near_ref[...] = jnp.zeros_like(near_ref)
+    for step, piece in zip(steps, pieces):
+        add_piece(axis, groups, piece, step, near_ref)
     for copy in copies:
         copy.wait()
     for phase in range(taps_ref.shape[0]):
@@ -386,41 +394,42 @@
             spread_ref[phase, j] = jnp.broadcast_to(taps_ref[phase, j : j + 1], (8, LANES))
 
 
-def fine_tables_section(fine_taps):
+def fine_tables_section(pieces, fine_taps, axis, groups):
     taps_count, fine = fine_taps.shape
     taps = fine_taps.reshape(taps_count, LANES, fine // LANES).transpose(2, 0, 1)
     table, turns = fine_tables(fine)
     turns = np.repeat(turns[:, :, None, :], 8, axis=2)
     shape = (fine // LANES, taps_count, 8, LANES)
     return pl.pallas_call(
-        tables_kernel,
+        lambda *refs: tables_kernel(axis, groups, *refs),
         out_shape=[
             pltpu.VMEM(shape, F32),
             pltpu.VMEM((2, 2 * LANES, 2 * LANES), BF16),
             pltpu.VMEM(turns.shape, F32),
+            pltpu.VMEM((groups + 1, 2, 2 * LANES // groups, LANES), F32),
         ],
-        in_specs=[ANY] * 3,
-        out_specs=[VMEM] * 3,
+        in_specs=[ANY] * 3 + [VMEM] * len(pieces),
+        out_specs=[VMEM] * 4,
         scratch_shapes=[pltpu.VMEM(taps.shape, F32), pltpu.SemaphoreType.DMA((3,))],
         compiler_params=PARAMS,
         cost_estimate=COST,
         name="tables",
-    )(taps, in_hbm(jnp.asarray(np.stack(split_table(table)))), in_hbm(jnp.asarray(turns)))
-
-
-def fine_begin(pieces, taps, axis, groups, shares):
+    )(taps, in_hbm(jnp.asarray(np.stack(split_table(table)))), in_hbm(jnp.asarray(turns)), *map(in_vmem, pieces))
+
+
+def fine_begin(pieces, near, taps, axis, groups, shares):
     span = 2 * LANES // groups
     per, frames = span // (4 * shares), 2 * groups
     acc = pl.pallas_call(
         lambda *refs: fine_start_kernel(axis, groups, shares, *refs),
         out_shape=pltpu.VMEM((shares, 4, 2, frames * per, LANES), F32),
-        in_specs=[VMEM] * (1 + groups),
+        in_specs=[VMEM] * (2 + len(pieces)),
         out_specs=VMEM,
         scratch_shapes=[pltpu.VMEM((groups + 1, 2, span, LANES), F32)],
         compiler_params=PARAMS,
         cost_estimate=COST,
         name="fine_start",
-    )(in_vmem(taps), *[in_vmem(value) for value in pieces])
+    )(in_vmem(taps), in_vmem(near), *[in_vmem(value) for value in pieces])
     return acc
 
 
@@ -470,12 +479,12 @@
         late = [swap(second[1 + step], step) for step in range(2, groups)]
         beside = swap(second[2], 1)
         moved = [[second[1], beside] + late]
-        pieces = [second[0], beside]
+        relayed = []
         for value in reached:
             half = value[value.shape[0] // 2 - 4 :]
-            pieces += [value, swap(half, 1)]
-        tables = fine_tables_section(fine_taps)
-        acc = fine_begin(pieces, tables[0], axis, groups, shares)
+            relayed.append(swap(half, 1))
+        *tables, near = fine_tables_section([second[0], beside, *reached], fine_taps, axis, groups)
+        acc = fine_begin(relayed, near, tables[0], axis, groups, shares)
         return fine_section(moved, tables, acc, axis, groups, shares)
 
     return jax.shard_map(

time: 15.7 us -> 15.7 us (level)
  no operation moved by 1% of the time
where the time goes in v6:
time: 15.7 us; the launch traced here: 15.5 us
  waiting for transfers between devices  5.23 us (33%)
  starting transfers between devices  4.99 us (32%)
  Pallas kernels  4.94 us (31%)
  local copies, waits for them, and re-layouts  0.25 us (2%)
    ppermute x5, waiting for transfers between devices, swap(): return lax.ppermute(value, axis, [(i, i ^ step) for i in range(groups)])  5.23 us
    ppermute x5, starting transfers between devices, swap(): return lax.ppermute(value, axis, [(i, i ^ step) for i in range(groups)])  4.99 us
    pallas_call x1, Pallas kernels, coarse_section(): pl.pallas_call(lambda *refs: coarse_kernel(axis, groups, *refs), out_shap...  1.6 us
    pallas_call x1, Pallas kernels, fine_section(): pl.pallas_call(lambda *refs: fine_kernel(axis, groups, shares, share, *re...  1.36 us
    pallas_call x1, Pallas kernels, fine_tables_section(): pl.pallas_call(lambda *refs: tables_kernel(axis, groups, *refs), out_shap...  1.04 us
    pallas_call x1, Pallas kernels, coarse_section(): pl.pallas_call(lambda *refs: coarse_rest_kernel(axis, groups, *refs), out...  0.69 us
  transfers between devices with their start and end apart: 5, of which 3 were waited for; matrix products, arithmetic and copies ran while one was open for 2% of the time, Pallas kernels for 13%

profile of v6, /device:TPU:0, one launch (start us, length us, event | category | flops | bytes accessed | tf_op | source)
XLA Modules:
  0.0 15.5 jit_solution(12340289334924908473)
XLA Ops:
  0.0 1.6 %coarse.1 = (f32[264,128]{1,0:T(8,128)S(1)}, bf16[256,256]{1,0:T(8,128)(2,1)S(1)}, bf16[256,256]{1,0:T(8,128)(2,1)S(1)}, bf16[16,256]{1,0:T(8,128)(2,1)S(1)}, bf...) custom-call(f32[1024,128]{1,0:T(8,128)} %bitcast.14, ...), custom_call_target="tpu_custom_call" | custom-call | flops 2000000 | bytes 1000000 | tf_op jit(solution)/shard_map/coarse/pallas_call | solution.py:221
  1.6 3.1 %collective-permute-start.1 = (f32[264,128]{1,0:T(8,128)S(1)}, f32[264,128]{1,0:T(8,128)S(1)}, u32[]{:S(2)}, u32[]{:S(2)}) collective-permute-start(f32[264,128]{1,0:T(8,128)S(1)} %get-tuple-element.31), channel_id=1, source_target_pairs={{0,2},{1,3},{2,0},{3,1},{4,6},{5,7},{6,4},{7,5},{8,10},{9,11},{10,... | collective-permute-start | bytes 405512 | tf_op jit(solution)/shard_map/ppermute | solution.py:473
  4.7 0.7 %coarse_rest.1 = (f32[136,128]{1,0:T(8,128)S(1)}, f32[128,128]{1,0:T(8,128)S(1)}, f32[264,128]{1,0:T(8,128)S(1)}, f32[128,128]{1,0:T(8,128)S(1)}, f32[128,128]{1,0:T(8,128)S(1)}) custom-call(bf16[256,256]{1,0:T(8,128)(2,1)S(1)} %get-tuple-element.22.refs_0_, bf16[256,256]{1,0:T(8,128)(2,1)S(1)} %get-tuple-element.23.refs_1_, ...), custom_call_target="tpu_custom_call" | custom-call | flops 2000000 | bytes 1000000 | tf_op jit(solution)/shard_map/coarse_rest/pallas_call | solution.py:247
  5.4 0.0 copy-start
  5.4 0.1 collective-permute-start
  5.5 2.8 %collective-permute-done.1.refs_5_ = f32[264,128]{1,0:T(8,128)S(1)} collective-permute-done((f32[264,128]{1,0:T(8,128)S(1)}, f32[264,128]{1,0:T(8,128)S(1)}, u32[]{:S(2)}, u32[]{:S(2)}) %collective-permute-start.1) | collective-permute-done | bytes 135200 | tf_op jit(solution)/shard_map/ppermute | solution.py:473
  8.3 0.0 collective-permute-start.2
  8.3 1.8 %collective-permute-start.3 = (f32[128,128]{1,0:T(8,128)S(1)}, f32[128,128]{1,0:T(8,128)S(1)}, u32[]{:S(2)}, u32[]{:S(2)}) collective-permute-start(f32[128,128]{1,0:T(8,128)S(1)} %get-tuple-element.37), channel_id=1, source_target_pairs={{0,2},{1,3},{2,0},{3,1},{4,6},{5,7},{6,4},{7,5},{8,10},{9,11},{10,... | collective-permute-start | bytes 196616 | tf_op jit(solution)/shard_map/ppermute | solution.py:473
  10.1 0.0 collective-permute-start.4
  10.1 0.0 copy-done
  10.1 0.1 copy.8
  10.3 0.1 copy.9
  10.4 0.0 collective-permute-done.refs_4_.refs_5_
  10.4 1.0 %tables.1 = (f32[4,12,8,128]{3,2,1,0:T(8,128)S(1)}, bf16[2,256,256]{2,1,0:T(8,128)(2,1)S(1)}, f32[4,2,8,128]{3,2,1,0:T(8,128)S(1)}, f32[5,2,64,128]{3,2,1,0:T(8,128)S(1)}) custom-call(f32[4,12,128]{2,1,0:T(8,128)S(1)} %bitcast.12, bf16[2,256,256]{2,1,0:T(8,128)(2,1)} %constant.7.clone.refs_1_, f32[4,2,8,128]{3,2,1,0:T(8,128)} %constant.8.clone.refs_2_, ...), custom_call_target="tpu_custom_call" | custom-call | flops 2000000 | bytes 1000000 | tf_op jit(solution)/shard_map/tables/pallas_call | solution.py:403
  11.4 0.0 collective-permute-done.2.refs_2_
  11.4 0.2 %fine_start.1.refs_3_ = f32[1,4,2,128,128]{4,3,2,1,0:T(8,128)S(1)} custom-call(f32[4,12,8,128]{3,2,1,0:T(8,128)S(1)} %get-tuple-element.32.refs_0_, f32[5,2,64,128]{3,2,1,0:T(8,128)S(1)} %get-tuple-element.35.refs_1_, f32[136,128]{1,0:T(8,128)S(1)} %collective-permute-done.2.refs_2_), custom_call_target="tpu_custom_call" | custom-call | flops 2000000 | bytes 1000000 | tf_op jit(solution)/shard_map/fine_start/pallas_call | solution.py:423
  11.7 1.1 %collective-permute-done.3.refs_6_ = f32[128,128]{1,0:T(8,128)S(1)} collective-permute-done((f32[128,128]{1,0:T(8,128)S(1)}, f32[128,128]{1,0:T(8,128)S(1)}, u32[]{:S(2)}, u32[]{:S(2)}) %collective-permute-start.3) | collective-permute-done | bytes 65568 | tf_op jit(solution)/shard_map/ppermute | solution.py:473
  12.8 1.4 %collective-permute-done.4.refs_7_ = f32[128,128]{1,0:T(8,128)S(1)} collective-permute-done((f32[128,128]{1,0:T(8,128)S(1)}, f32[128,128]{1,0:T(8,128)S(1)}, u32[]{:S(2)}, u32[]{:S(2)}) %collective-permute-start.4) | collective-permute-done | bytes 65568 | tf_op jit(solution)/shard_map/ppermute | solution.py:473
  14.1 1.4 %fine.1 = f32[2,512,128]{2,1,0:T(8,128)} custom-call(f32[4,12,8,128]{3,2,1,0:T(8,128)S(1)} %get-tuple-element.32.refs_0_, bf16[2,256,256]{2,1,0:T(8,128)(2,1)S(1)} %get-tuple-element.33.refs_1_, f32[4,2,8,128]{3,2,1,0:T(8,128)S(1)} %get-tuple-element.34.refs_2_, f32[1,4,2,128,128]{4,3,2,1,0:T(8,128)S(1)} %fine_start.1.refs_3_, ...), custom_call_target="tpu_custom_call" | custom-call | flops 2000000 | bytes 1000000 | tf_op jit(solution)/shard_map/fine/pallas_call | solution.py:445
  (1 shorter events, 0.0 us)
Async XLA Ops:
  1.6 6.6 %collective-permute-start.1 = (f32[264,128]{1,0:T(8,128)S(1)}, f32[264,128]{1,0:T(8,128)S(1)}, u32[]{:S(2)}, u32[]{:S(2)}) collective-permute-start(f32[264,128]{1,0:T(8,128)S(1)} %get-tuple-element.31), channel_id=1, source_target_pairs={{0,2},{1,3},{2,0},{3,1},{4,6},{5,7},{6,4},{7,5},{8,10},{9,11},{10,... | collective-permute-start | bytes 405512 | tf_op jit(solution)/shard_map/ppermute | solution.py:473
  5.4 4.8 %copy-start = (f32[12,512]{1,0:T(8,128)S(1)}, f32[12,512]{1,0:T(8,128)}, u32[]{:S(2)}) copy-start(f32[12,512]{1,0:T(8,128)} %param.8) | copy-start | bytes 73732
  5.4 5.0 %collective-permute-start = (f32[264,128]{1,0:T(8,128)S(1)}, f32[264,128]{1,0:T(8,128)S(1)}, u32[]{:S(2)}, u32[]{:S(2)}) collective-permute-start(f32[264,128]{1,0:T(8,128)S(1)} %get-tuple-element.30), channel_id=1, source_target_pairs={{0,1},{1,0},{2,3},{3,2},{4,5},{5,4},{6,7},{7,6},{8,9},{9,8},{10,11... | collective-permute-start | bytes 405512 | tf_op jit(solution)/shard_map/ppermute | solution.py:473
  8.3 3.2 %collective-permute-start.2 = (f32[136,128]{1,0:T(8,128)S(1)}, f32[136,128]{1,0:T(8,128)S(1)}, u32[]{:S(2)}, u32[]{:S(2)}) collective-permute-start(f32[136,128]{1,0:T(8,128)S(1)} %slice.4), channel_id=1, source_target_pairs={{0,1},{1,0},{2,3},{3,2},{4,5},{5,4},{6,7},{7,6},{8,9},{9,8},{10,11... | collective-permute-start | bytes 208904 | tf_op jit(solution)/shard_map/ppermute | solution.py:473
  8.3 4.5 %collective-permute-start.3 = (f32[128,128]{1,0:T(8,128)S(1)}, f32[128,128]{1,0:T(8,128)S(1)}, u32[]{:S(2)}, u32[]{:S(2)}) collective-permute-start(f32[128,128]{1,0:T(8,128)S(1)} %get-tuple-element.37), channel_id=1, source_target_pairs={{0,2},{1,3},{2,0},{3,1},{4,6},{5,7},{6,4},{7,5},{8,10},{9,11},{10,... | collective-permute-start | bytes 196616 | tf_op jit(solution)/shard_map/ppermute | solution.py:473
  10.1 4.1 %collective-permute-start.4 = (f32[128,128]{1,0:T(8,128)S(1)}, f32[128,128]{1,0:T(8,128)S(1)}, u32[]{:S(2)}, u32[]{:S(2)}) collective-permute-start(f32[128,128]{1,0:T(8,128)S(1)} %get-tuple-element.38), channel_id=1, source_target_pairs={{0,3},{1,2},{2,1},{3,0},{4,7},{5,6},{6,5},{7,4},{8,11},{9,10},{10,... | collective-permute-start | bytes 196616 | tf_op jit(solution)/shard_map/ppermute | solution.py:473

commit v7 on v6

--- a/solution.py
+++ b/solution.py
@@ -375,23 +375,26 @@
         copy.wait()
 
 
-def tables_kernel(axis, groups, spread_hbm, table_hbm, turn_hbm, *refs):
-    steps = [0, 1, *range(2, groups, 2)]
-    pieces, (spread_ref, table_ref, turn_ref, near_ref, taps_ref, sems) = refs[: len(steps)], refs[len(steps) :]
+def constants_kernel(table_hbm, turn_hbm, table_ref, turn_ref, sems):
     copies = [
         pltpu.make_async_copy(source, target, sems.at[i])
-        for i, (source, target) in enumerate(((spread_hbm, taps_ref), (table_hbm, table_ref), (turn_hbm, turn_ref)))
+        for i, (source, target) in enumerate(((table_hbm, table_ref), (turn_hbm, turn_ref)))
     ]
     for copy in copies:
         copy.start()
+    for copy in copies:
+        copy.wait()
+
+
+def tables_kernel(axis, groups, taps_ref, *refs):
+    steps = [0, 1, *range(2, groups, 2)]
+    pieces, (spread_ref, near_ref) = refs[: len(steps)], refs[len(steps) :]
+    for phase in range(taps_ref.shape[0]):
+        for j in range(taps_ref.shape[1]):
+            spread_ref[phase, j] = jnp.broadcast_to(taps_ref[phase, j : j + 1], (8, LANES))
     near_ref[...] = jnp.zeros_like(near_ref)
     for step, piece in zip(steps, pieces):
         add_piece(axis, groups, piece, step, near_ref)
-    for copy in copies:
-        copy.wait()
-    for phase in range(taps_ref.shape[0]):
-        for j in range(taps_ref.shape[1]):
-            spread_ref[phase, j] = jnp.broadcast_to(taps_ref[phase, j : j + 1], (8, LANES))
 
 
 def fine_tables_section(pieces, fine_taps, axis, groups):
@@ -400,21 +403,26 @@
     table, turns = fine_tables(fine)
     turns = np.repeat(turns[:, :, None, :], 8, axis=2)
     shape = (fine // LANES, taps_count, 8, LANES)
-    return pl.pallas_call(
+    constants = pl.pallas_call(
+        constants_kernel,
+        out_shape=[pltpu.VMEM((2, 2 * LANES, 2 * LANES), BF16), pltpu.VMEM(turns.shape, F32)],
+        in_specs=[ANY] * 2,
+        out_specs=[VMEM] * 2,
+        scratch_shapes=[pltpu.SemaphoreType.DMA((2,))],
+        compiler_params=PARAMS,
+        cost_estimate=COST,
+        name="constants",
+    )(in_hbm(jnp.asarray(np.stack(split_table(table)))), in_hbm(jnp.asarray(turns)))
+    spread, near = pl.pallas_call(
         lambda *refs: tables_kernel(axis, groups, *refs),
-        out_shape=[
-            pltpu.VMEM(shape, F32),
-            pltpu.VMEM((2, 2 * LANES, 2 * LANES), BF16),
-            pltpu.VMEM(turns.shape, F32),
-            pltpu.VMEM((groups + 1, 2, 2 * LANES // groups, LANES), F32),
-        ],
-        in_specs=[ANY] * 3 + [VMEM] * len(pieces),
-        out_specs=[VMEM] * 4,
-        scratch_shapes=[pltpu.VMEM(taps.shape, F32), pltpu.SemaphoreType.DMA((3,))],
+        out_shape=[pltpu.VMEM(shape, F32), pltpu.VMEM((groups + 1, 2, 2 * LANES // groups, LANES), F32)],
+        in_specs=[VMEM] * (1 + len(pieces)),
+        out_specs=[VMEM] * 2,
         compiler_params=PARAMS,
         cost_estimate=COST,
         name="tables",
-    )(taps, in_hbm(jnp.asarray(np.stack(split_table(table)))), in_hbm(jnp.asarray(turns)), *map(in_vmem, pieces))
+    )(in_vmem(taps), *map(in_vmem, pieces))
+    return [spread, *constants, near]
 
 
 def fine_begin(pieces, near, taps, axis, groups, shares):

time: 15.7 us -> 15.7 us (level)
    pallas_call x0 -> x1, Pallas kernels: none -> 1 us  [fine_tables_section(): pl.pallas_call(constants_kernel, out_shape=[pltpu.VMEM((2, 2 * LANES, 2 *...]
    pallas_call x1, Pallas kernels: 1.04 us -> 0.18 us  [fine_tables_section(): pl.pallas_call(lambda *refs: tables_kernel(axis, groups, *refs), out_shap...]
  transfers between devices with their start and end apart: 5 -> 5, of which waited for: 3 -> 3; matrix products, arithmetic and copies ran while one was open for 2% -> 2% of each run, Pallas kernels for 13% -> 14%
where the time goes in v7:
time: 15.7 us; the launch traced here: 15.5 us
  Pallas kernels  5.08 us (32%)
  waiting for transfers between devices  5.08 us (32%)
  starting transfers between devices  4.99 us (32%)
  local copies, waits for them, and re-layouts  0.25 us (2%)
    ppermute x5, waiting for transfers between devices, swap(): return lax.ppermute(value, axis, [(i, i ^ step) for i in range(groups)])  5.08 us
    ppermute x5, starting transfers between devices, swap(): return lax.ppermute(value, axis, [(i, i ^ step) for i in range(groups)])  4.99 us
    pallas_call x1, Pallas kernels, coarse_section(): pl.pallas_call(lambda *refs: coarse_kernel(axis, groups, *refs), out_shap...  1.6 us
    pallas_call x1, Pallas kernels, fine_section(): pl.pallas_call(lambda *refs: fine_kernel(axis, groups, shares, share, *re...  1.36 us
    pallas_call x1, Pallas kernels, fine_tables_section(): pl.pallas_call(constants_kernel, out_shape=[pltpu.VMEM((2, 2 * LANES, 2 *...  1 us
    pallas_call x1, Pallas kernels, coarse_section(): pl.pallas_call(lambda *refs: coarse_rest_kernel(axis, groups, *refs), out...  0.69 us
  transfers between devices with their start and end apart: 5, of which 3 were waited for; matrix products, arithmetic and copies ran while one was open for 2% of the time, Pallas kernels for 14%

profile of v7, /device:TPU:0, one launch (start us, length us, event | category | flops | bytes accessed | tf_op | source)
XLA Modules:
  0.0 15.5 jit_solution(17686773711166367265)
XLA Ops:
  0.0 1.6 %coarse.1 = (f32[264,128]{1,0:T(8,128)S(1)}, bf16[256,256]{1,0:T(8,128)(2,1)S(1)}, bf16[256,256]{1,0:T(8,128)(2,1)S(1)}, bf16[16,256]{1,0:T(8,128)(2,1)S(1)}, bf...) custom-call(f32[1024,128]{1,0:T(8,128)} %bitcast.14, ...), custom_call_target="tpu_custom_call" | custom-call | flops 2000000 | bytes 1000000 | tf_op jit(solution)/shard_map/coarse/pallas_call | solution.py:221
  1.6 3.1 %collective-permute-start.1 = (f32[264,128]{1,0:T(8,128)S(1)}, f32[264,128]{1,0:T(8,128)S(1)}, u32[]{:S(2)}, u32[]{:S(2)}) collective-permute-start(f32[264,128]{1,0:T(8,128)S(1)} %get-tuple-element.31), channel_id=1, source_target_pairs={{0,2},{1,3},{2,0},{3,1},{4,6},{5,7},{6,4},{7,5},{8,10},{9,11},{10,... | collective-permute-start | bytes 405512 | tf_op jit(solution)/shard_map/ppermute | solution.py:481
  4.7 0.7 %coarse_rest.1 = (f32[136,128]{1,0:T(8,128)S(1)}, f32[128,128]{1,0:T(8,128)S(1)}, f32[264,128]{1,0:T(8,128)S(1)}, f32[128,128]{1,0:T(8,128)S(1)}, f32[128,128]{1,0:T(8,128)S(1)}) custom-call(bf16[256,256]{1,0:T(8,128)(2,1)S(1)} %get-tuple-element.22.refs_0_, bf16[256,256]{1,0:T(8,128)(2,1)S(1)} %get-tuple-element.23.refs_1_, ...), custom_call_target="tpu_custom_call" | custom-call | flops 2000000 | bytes 1000000 | tf_op jit(solution)/shard_map/coarse_rest/pallas_call | solution.py:247
  5.4 0.0 copy-start
  5.4 0.1 collective-permute-start
  5.5 2.8 %collective-permute-done.1.refs_3_ = f32[264,128]{1,0:T(8,128)S(1)} collective-permute-done((f32[264,128]{1,0:T(8,128)S(1)}, f32[264,128]{1,0:T(8,128)S(1)}, u32[]{:S(2)}, u32[]{:S(2)}) %collective-permute-start.1) | collective-permute-done | bytes 135200 | tf_op jit(solution)/shard_map/ppermute | solution.py:481
  8.3 0.0 collective-permute-start.2
  8.3 1.8 %collective-permute-start.3 = (f32[128,128]{1,0:T(8,128)S(1)}, f32[128,128]{1,0:T(8,128)S(1)}, u32[]{:S(2)}, u32[]{:S(2)}) collective-permute-start(f32[128,128]{1,0:T(8,128)S(1)} %get-tuple-element.37), channel_id=1, source_target_pairs={{0,2},{1,3},{2,0},{3,1},{4,6},{5,7},{6,4},{7,5},{8,10},{9,11},{10,... | collective-permute-start | bytes 196616 | tf_op jit(solution)/shard_map/ppermute | solution.py:481
  10.1 0.0 collective-permute-start.4
  10.1 0.0 copy-done
  10.1 0.1 copy.8
  10.3 0.1 copy.9
  10.4 1.0 %constants.1 = (bf16[2,256,256]{2,1,0:T(8,128)(2,1)S(1)}, f32[4,2,8,128]{3,2,1,0:T(8,128)S(1)}) custom-call(bf16[2,256,256]{2,1,0:T(8,128)(2,1)} %constant.7.clone.table_hbm, f32[4,2,8,128]{3,2,1,0:T(8,128)} %constant.8.clone.turn_hbm), custom_call_target="tpu_custom_call" | custom-call | flops 2000000 | bytes 1000000 | tf_op jit(solution)/shard_map/constants/pallas_call | solution.py:406
  11.4 0.0 collective-permute-done.refs_2_.refs_5_
  11.4 0.2 %tables.1 = (f32[4,12,8,128]{3,2,1,0:T(8,128)S(1)}, f32[5,2,64,128]{3,2,1,0:T(8,128)S(1)}) custom-call(f32[4,12,128]{2,1,0:T(8,128)S(1)} %bitcast.12, f32[136,128]{1,0:T(8,128)S(1)} %get-tuple-element.29.refs_1_, f32[264,128]{1,0:T(8,128)S(1)} %collective-permute-done.refs_2_.refs_5_, f32[264,128]{1,0:T(8,128)S(1)} %collective-permute-done.1.refs_3_), custom_call_target="tpu_custom_call" | custom-call | flops 2000000 | bytes 1000000 | tf_op jit(solution)/shard_map/tables/pallas_call | solution.py:416
  11.6 0.0 collective-permute-done.2.refs_2_
  11.6 0.2 %fine_start.1.refs_3_ = f32[1,4,2,128,128]{4,3,2,1,0:T(8,128)S(1)} custom-call(f32[4,12,8,128]{3,2,1,0:T(8,128)S(1)} %get-tuple-element.32.refs_0_, f32[5,2,64,128]{3,2,1,0:T(8,128)S(1)} %get-tuple-element.35.refs_1_, f32[136,128]{1,0:T(8,128)S(1)} %collective-permute-done.2.refs_2_), custom_call_target="tpu_custom_call" | custom-call | flops 2000000 | bytes 1000000 | tf_op jit(solution)/shard_map/fine_start/pallas_call | solution.py:431
  11.8 0.9 %collective-permute-done.3.refs_6_ = f32[128,128]{1,0:T(8,128)S(1)} collective-permute-done((f32[128,128]{1,0:T(8,128)S(1)}, f32[128,128]{1,0:T(8,128)S(1)}, u32[]{:S(2)}, u32[]{:S(2)}) %collective-permute-start.3) | collective-permute-done | bytes 65568 | tf_op jit(solution)/shard_map/ppermute | solution.py:481
  12.8 1.4 %collective-permute-done.4.refs_7_ = f32[128,128]{1,0:T(8,128)S(1)} collective-permute-done((f32[128,128]{1,0:T(8,128)S(1)}, f32[128,128]{1,0:T(8,128)S(1)}, u32[]{:S(2)}, u32[]{:S(2)}) %collective-permute-start.4) | collective-permute-done | bytes 65568 | tf_op jit(solution)/shard_map/ppermute | solution.py:481
  14.1 1.4 %fine.1 = f32[2,512,128]{2,1,0:T(8,128)} custom-call(f32[4,12,8,128]{3,2,1,0:T(8,128)S(1)} %get-tuple-element.32.refs_0_, bf16[2,256,256]{2,1,0:T(8,128)(2,1)S(1)} %get-tuple-element.33.refs_1_, f32[4,2,8,128]{3,2,1,0:T(8,128)S(1)} %get-tuple-element.34.refs_2_, f32[1,4,2,128,128]{4,3,2,1,0:T(8,128)S(1)} %fine_start.1.refs_3_, ...), custom_call_target="tpu_custom_call" | custom-call | flops 2000000 | bytes 1000000 | tf_op jit(solution)/shard_map/fine/pallas_call | solution.py:453
  (1 shorter events, 0.0 us)
Async XLA Ops:
  1.6 6.6 %collective-permute-start.1 = (f32[264,128]{1,0:T(8,128)S(1)}, f32[264,128]{1,0:T(8,128)S(1)}, u32[]{:S(2)}, u32[]{:S(2)}) collective-permute-start(f32[264,128]{1,0:T(8,128)S(1)} %get-tuple-element.31), channel_id=1, source_target_pairs={{0,2},{1,3},{2,0},{3,1},{4,6},{5,7},{6,4},{7,5},{8,10},{9,11},{10,... | collective-permute-start | bytes 405512 | tf_op jit(solution)/shard_map/ppermute | solution.py:481
  5.4 4.8 %copy-start = (f32[12,512]{1,0:T(8,128)S(1)}, f32[12,512]{1,0:T(8,128)}, u32[]{:S(2)}) copy-start(f32[12,512]{1,0:T(8,128)} %param.8) | copy-start | bytes 73732
  5.4 6.0 %collective-permute-start = (f32[264,128]{1,0:T(8,128)S(1)}, f32[264,128]{1,0:T(8,128)S(1)}, u32[]{:S(2)}, u32[]{:S(2)}) collective-permute-start(f32[264,128]{1,0:T(8,128)S(1)} %get-tuple-element.30), channel_id=1, source_target_pairs={{0,1},{1,0},{2,3},{3,2},{4,5},{5,4},{6,7},{7,6},{8,9},{9,8},{10,11... | collective-permute-start | bytes 405512 | tf_op jit(solution)/shard_map/ppermute | solution.py:481
  8.3 3.3 %collective-permute-start.2 = (f32[136,128]{1,0:T(8,128)S(1)}, f32[136,128]{1,0:T(8,128)S(1)}, u32[]{:S(2)}, u32[]{:S(2)}) collective-permute-start(f32[136,128]{1,0:T(8,128)S(1)} %slice.4), channel_id=1, source_target_pairs={{0,1},{1,0},{2,3},{3,2},{4,5},{5,4},{6,7},{7,6},{8,9},{9,8},{10,11... | collective-permute-start | bytes 208904 | tf_op jit(solution)/shard_map/ppermute | solution.py:481
  8.3 4.5 %collective-permute-start.3 = (f32[128,128]{1,0:T(8,128)S(1)}, f32[128,128]{1,0:T(8,128)S(1)}, u32[]{:S(2)}, u32[]{:S(2)}) collective-permute-start(f32[128,128]{1,0:T(8,128)S(1)} %get-tuple-element.37), channel_id=1, source_target_pairs={{0,2},{1,3},{2,0},{3,1},{4,6},{5,7},{6,4},{7,5},{8,10},{9,11},{10,... | collective-permute-start | bytes 196616 | tf_op jit(solution)/shard_map/ppermute | solution.py:481
  10.1 4.1 %collective-permute-start.4 = (f32[128,128]{1,0:T(8,128)S(1)}, f32[128,128]{1,0:T(8,128)S(1)}, u32[]{:S(2)}, u32[]{:S(2)}) collective-permute-start(f32[128,128]{1,0:T(8,128)S(1)} %get-tuple-element.38), channel_id=1, source_target_pairs={{0,3},{1,2},{2,1},{3,0},{4,7},{5,6},{6,5},{7,4},{8,11},{9,10},{10,... | collective-permute-start | bytes 196616 | tf_op jit(solution)/shard_map/ppermute | solution.py:481
